TPU v7x, 32 devices: a whole 2x2x4 slice. The times are simulated.
32 devices in a mesh: dp: 4 (over x, core), expert: 8 (over z, y).
Axes of the slice: x: 2, y: 2, z: 4, core: 2. Of those that a mesh axis runs over, the one named last changes fastest.
Arguments:
- hidden_in: bfloat16 [8192, 2, 768], P(('dp', 'expert')), may hold values from -6 to 6
- cotangent: bfloat16 [8192, 2, 768], P(('dp', 'expert')), may hold values from -6 to 6
- gate_residual: float32 [8192, 2, 12], P(('dp', 'expert')), may hold values from -6 to 6
- routes: int32 [8192, 2, 2], P(('dp', 'expert')), may hold values from 0 to 11, all different within a row; in each aligned block of 512 rows (0 to 511, 512 to 1023, ..., all dimensions but the last counted through in order) at most 128 rows name the same one
- groups: int32 [32], P('dp'), may hold values from 0 to 0, as said below
- lengths: int32 [32], P('dp'), may hold values from 1 to 256, 6144 in all
- attn_gain: bfloat16 [768], P(('dp', 'expert')), may hold values from 0.5 to 1.5
- qkv_weight: bfloat16 [768, 2304], P(('dp', 'expert')), may hold values from -0.21875 to 0.21875
- out_weight: bfloat16 [768, 768], P(('dp', 'expert')), may hold values from -1.75 to 1.75
- ffn_gain: bfloat16 [768], P(('dp', 'expert')), may hold values from 0.5 to 1.5
- router_weight: bfloat16 [768, 12], P(('dp', 'expert')), may hold values from -0.21875 to 0.21875
- const_proj: bfloat16 [768, 4], P(('dp', 'expert')), may hold values from -0.21875 to 0.21875
- const_vec: bfloat16 [768, 2], P(('dp', 'expert')), may hold values from -6 to 6
- gate_weight: bfloat16 [768, 16384], P('dp', 'expert'), may hold values from -0.21875 to 0.21875
- up_weight: bfloat16 [768, 16384], P('dp', 'expert'), may hold values from -0.21875 to 0.21875
- down_weight: bfloat16 [768, 16384], P('dp', 'expert'), may hold values from -0.375 to 0.375
Outputs:
- output: bfloat16 [8192, 2, 768], P(('dp', 'expert'))
- grad_input: float32 [8192, 2, 768], P(('dp', 'expert'))
- grad_gate_residual: float32 [8192, 2, 12], P(('dp', 'expert'))
- grad_attn_gain: float32 [768], P(('dp', 'expert'))
- grad_qkv_weight: float32 [768, 2304], P(('dp', 'expert'))
- grad_out_weight: float32 [768, 768], P(('dp', 'expert'))
- grad_ffn_gain: float32 [768], P(('dp', 'expert'))
- grad_router_weight: float32 [768, 12], P(('dp', 'expert'))
- grad_const_proj: float32 [768, 4], P(('dp', 'expert'))
- grad_const_vec: float32 [768, 2], P(('dp', 'expert'))
- grad_gate_weight: float32 [768, 16384], P('dp', 'expert')
- grad_up_weight: float32 [768, 16384], P('dp', 'expert')
- grad_down_weight: float32 [768, 16384], P('dp', 'expert')
Inputs may be any that keep to these rules, and one draw needn't show every extreme that they name: `routes`: among the 512 rows of one device (aligned blocks of 256 first-dimension indices), no number is named by more than 128 rows; each row names two different numbers; number 8 is the zero expert, 9 the copy expert, 10 and 11 the constant experts. `groups`: in each aligned block of 8 continuations (one index of dp) every prompt number is named by exactly 8 of them.
All inputs are finite; a program needn't handle non-finite values. No bound on the sum of `lengths` on one device may be relied on, other than what follows from the above.
Results may differ from a plain program's by a relative error of at most 0.022.
Values may be sent and summed in bfloat16 or wider, within the bound.
No kernel may reach another device: no remote copies, remote signals or barrier semaphores. Data moves between devices by JAX's collectives and lax.ppermute only.
A program may use at most 256 MiB of HBM per device.

v0:
```python
import math

import jax
import jax.numpy as jnp
from jax import lax
from jax.sharding import PartitionSpec as P

D = 768
HEADS = 12
HEAD_DIM = 64
EXPERTS = 8
CONT_LEN = 256
PROMPT = 2048


epsilon = 1e-06
negative = -1e30
top_precision = lax.Precision.HIGHEST


def rms_scale(value_matrix, gain):
    return (
        value_matrix
        * lax.rsqrt(jnp.mean(value_matrix * value_matrix, axis=-1, keepdims=True) + epsilon)
        * gain
    )


def rotate(value_matrix, position):
    half_width = value_matrix.shape[-1] // 2
    frequency = 10000.0 ** (-jnp.arange(half_width, dtype=jnp.float32) / half_width)
    angles = position[:, None, None] * frequency[None, None, :]
    cosine = jnp.cos(angles)
    sine_part = jnp.sin(angles)
    first_half = value_matrix[..., :half_width]
    second = value_matrix[..., half_width:]
    return jnp.concatenate(
        [first_half * cosine - second * sine_part, first_half * sine_part + second * cosine],
        axis=-1,
    )


def row_info(row_ids, kind_ids, length_table, prompt_table):
    matches = (row_ids // CONT_LEN)[:, None] == jnp.arange(length_table.shape[0], dtype=jnp.int32)[
        None, :
    ]
    length = jnp.sum(jnp.where(matches, length_table[None, :], 0), axis=1)
    prompt_of = jnp.sum(jnp.where(matches, prompt_table[None, :], 0), axis=1)
    sequence = jnp.where(kind_ids == 0, row_ids // PROMPT, row_ids // CONT_LEN)
    placement = jnp.where(kind_ids == 0, row_ids % PROMPT, row_ids % CONT_LEN)
    return (kind_ids, sequence, placement, length, prompt_of)


def visible(query_info, key_info):
    query_prompt = query_info[0][:, None] == 0
    key_prompt = key_info[0][None, :] == 0
    same_seq = query_info[1][:, None] == key_info[1][None, :]
    causal = key_info[2][None, :] <= query_info[2][:, None]
    prompt_self = query_prompt & key_prompt & same_seq & causal
    to_prompt = ~query_prompt & key_prompt & (key_info[1][None, :] == query_info[4][:, None])
    live_key = key_info[2][None, :] < key_info[3][None, :]
    own_part = ~query_prompt & ~key_prompt & same_seq & causal & live_key
    return prompt_self | to_prompt | own_part


def mix_part(picked, normed, normed_low, router_w, proj_w, vec_w, residual_logits, expert_rows):
    logits = jnp.dot(normed_low, router_w, precision=top_precision) + residual_logits
    route_probs = jax.nn.softmax(logits, axis=-1)
    one_hot = (
        picked[:, :, None] == jnp.arange(route_probs.shape[-1], dtype=jnp.int32)[None, None, :]
    ).astype(jnp.float32)
    mix_weight = jnp.sum(route_probs[:, None, :] * one_hot, axis=-1)
    const_logits = jnp.dot(normed_low, proj_w, precision=top_precision).reshape(-1, 2, 2)
    const_mix = jax.nn.softmax(const_logits, axis=-1)
    const_out = (
        const_mix[:, :, 0:1] * normed[:, None, :]
        + const_mix[:, :, 1:2] * jnp.transpose(vec_w)[None, :, :]
    )
    copy_term = jnp.where(picked[:, :, None] == EXPERTS + 1, normed[:, None, :], 0.0)
    first_const = jnp.where(picked[:, :, None] == EXPERTS + 2, const_out[:, 0:1, :], 0.0)
    second_const = jnp.where(picked[:, :, None] == EXPERTS + 3, const_out[:, 1:2, :], 0.0)
    branch = expert_rows + copy_term + first_const + second_const
    return jnp.sum(mix_weight[:, :, None] * branch, axis=1)


def contract_rows(left, right):
    return lax.dot_general(
        left, right, (((0,), (0,)), ((), ())), preferred_element_type=jnp.float32
    )


def contract_cols(left, right):
    return lax.dot_general(
        left, right, (((1,), (1,)), ((), ())), preferred_element_type=jnp.float32
    )


def per_device(
    hidden_in,
    cotangent,
    gate_residual,
    routes,
    groups,
    lengths,
    attn_gain,
    qkv_weight,
    out_weight,
    ffn_gain,
    router_weight,
    const_proj,
    const_vec,
    gate_weight,
    up_weight,
    down_weight,
):
    row_count = hidden_in.shape[0]
    pair_count = 2 * row_count
    capacity = row_count // 2
    owners = lax.axis_size("expert")
    copies = owners // EXPERTS
    my_index = lax.axis_index("expert")
    query_key_scale = float(HEAD_DIM) ** (-0.5)
    dense = (
        lax.all_gather(attn_gain, ("dp", "expert"), axis=0, tiled=True),
        lax.all_gather(qkv_weight, ("dp", "expert"), axis=0, tiled=True),
        lax.all_gather(out_weight, ("dp", "expert"), axis=0, tiled=True),
        lax.all_gather(ffn_gain, ("dp", "expert"), axis=0, tiled=True),
        lax.all_gather(router_weight, ("dp", "expert"), axis=0, tiled=True),
        lax.all_gather(const_proj, ("dp", "expert"), axis=0, tiled=True),
        lax.all_gather(const_vec, ("dp", "expert"), axis=0, tiled=True),
    )
    gain_one = dense[0].astype(jnp.float32)
    qkv_w = dense[1]
    out_w = dense[2]
    gain_two = dense[3].astype(jnp.float32)
    router_f = dense[4].astype(jnp.float32)
    proj_f = dense[5].astype(jnp.float32)
    vec_f = dense[6].astype(jnp.float32)
    expert_w = (
        lax.all_gather(gate_weight, "dp", axis=0, tiled=True),
        lax.all_gather(up_weight, "dp", axis=0, tiled=True),
        lax.all_gather(down_weight, "dp", axis=0, tiled=True),
    )
    gate_w = expert_w[0]
    up_w = expert_w[1]
    down_w = expert_w[2]
    width_local = gate_w.shape[1]
    flat_rows = jnp.repeat(my_index * row_count + jnp.arange(row_count, dtype=jnp.int32), 2)
    flat_kinds = jnp.tile(jnp.arange(2, dtype=jnp.int32), row_count)
    own_info = row_info(flat_rows, flat_kinds, lengths, groups)
    position = jnp.where(flat_kinds == 0, flat_rows % PROMPT, PROMPT + flat_rows % CONT_LEN).astype(
        jnp.float32
    )
    x_flat = hidden_in.reshape(pair_count, D).astype(jnp.float32)
    normed_one = rms_scale(x_flat, gain_one)
    normed_one_low = normed_one.astype(jnp.bfloat16)
    qkv = jnp.dot(normed_one_low, qkv_w, preferred_element_type=jnp.float32)
    query_matrix = rotate(qkv[:, :D].reshape(pair_count, HEADS, HEAD_DIM), position).astype(
        jnp.bfloat16
    )
    keys_rot = rotate(qkv[:, D : 2 * D].reshape(pair_count, HEADS, HEAD_DIM), position).astype(
        jnp.bfloat16
    )
    values_low = qkv[:, 2 * D :].reshape(pair_count, HEADS, HEAD_DIM).astype(jnp.bfloat16)
    kv_local = jnp.concatenate(
        [keys_rot.reshape(pair_count, D), values_low.reshape(pair_count, D)], axis=1
    ).reshape(row_count, 4 * D)

    def key_side_info(first_row, offset, step_rows):
        row_ids = jnp.repeat(first_row + offset + jnp.arange(step_rows, dtype=jnp.int32), 2)
        kind_ids = jnp.tile(jnp.arange(2, dtype=jnp.int32), step_rows)
        return row_info(row_ids, kind_ids, lengths, groups)

    start_state = (
        jnp.full((HEADS, pair_count), negative, jnp.float32),
        jnp.zeros((HEADS, pair_count), jnp.float32),
        jnp.zeros((HEADS, pair_count, HEAD_DIM), jnp.float32),
    )
    running = start_state
    piece = lax.all_gather(kv_local, "expert", axis=0, tiled=True)
    first_row = jnp.int32(0)
    piece_rows = piece.shape[0]
    step_rows = math.gcd(piece_rows, 256)
    key_blocks = piece.reshape(piece_rows // step_rows, step_rows, 4 * D)
    offsets = jnp.arange(piece_rows // step_rows, dtype=jnp.int32) * step_rows

    def fold_one_block(state, element):
        key_block, offset = element
        seen_mask = visible(own_info, key_side_info(first_row, offset, step_rows))

        def fold_compute(state):
            running_max, weight_sum, accumulated = state
            key_value_heads = key_block.reshape(2 * step_rows, 2, HEADS, HEAD_DIM)
            score_matrix = (
                jnp.einsum(
                    "stc,atc->tsa",
                    query_matrix,
                    key_value_heads[:, 0],
                    preferred_element_type=jnp.float32,
                )
                * query_key_scale
            )
            score_matrix = jnp.where(seen_mask[None], score_matrix, negative)
            new_max = jnp.maximum(running_max, jnp.max(score_matrix, axis=-1))
            weight_matrix = jnp.where(
                seen_mask[None], jnp.exp(score_matrix - new_max[:, :, None]), 0.0
            )
            factor = jnp.exp(running_max - new_max)
            weight_sum = weight_sum * factor + jnp.sum(weight_matrix, axis=-1)
            accumulated = accumulated * factor[:, :, None] + jnp.einsum(
                "rus,srb->rub",
                weight_matrix.astype(jnp.bfloat16),
                key_value_heads[:, 1],
                preferred_element_type=jnp.float32,
            )
            return (new_max, weight_sum, accumulated)

        return (lax.cond(jnp.any(seen_mask), fold_compute, lambda state: state, state), None)

    running, _ = lax.scan(fold_one_block, running, (key_blocks, offsets))
    running_max, weight_sum, accumulated = running
    attended = jnp.transpose(accumulated / weight_sum[:, :, None], (1, 0, 2))
    log_total = running_max + jnp.log(weight_sum)
    attended_low = attended.reshape(pair_count, D).astype(jnp.bfloat16)
    hidden = x_flat + jnp.dot(attended_low, out_w, preferred_element_type=jnp.float32)
    normed_two = rms_scale(hidden, gain_two)
    normed_two_low = normed_two.astype(jnp.bfloat16)
    picked = routes.reshape(pair_count, 2)
    flat_picked = picked.reshape(2 * pair_count)
    one_hot = (flat_picked[:, None] == jnp.arange(EXPERTS + 4, dtype=jnp.int32)[None, :]).astype(
        jnp.int32
    )
    slot_index = jnp.sum((jnp.cumsum(one_hot, axis=0) - one_hot) * one_hot, axis=1)
    is_expert = flat_picked < EXPERTS
    target = jnp.where(is_expert, flat_picked * capacity + slot_index, -1)
    take_index = jnp.where(is_expert, target, 0)
    placement = (
        jnp.arange(EXPERTS * capacity, dtype=jnp.int32)[:, None] == target[None, :]
    ).astype(jnp.bfloat16)

    def to_owners(slot_rows):
        shaped = slot_rows.reshape(EXPERTS, 1, capacity, D)
        return jnp.broadcast_to(shaped, (EXPERTS, copies, capacity, D)).reshape(owners, capacity, D)

    send_rows = jnp.dot(
        placement, jnp.repeat(normed_two_low, 2, axis=0), preferred_element_type=jnp.float32
    ).astype(jnp.bfloat16)
    received = lax.all_to_all(
        to_owners(send_rows), "expert", split_axis=0, concat_axis=0, tiled=True
    )
    item_count = received.shape[1]
    flat_in = received.reshape(owners * item_count, D)
    gate_pre = jnp.dot(flat_in, gate_w, preferred_element_type=jnp.float32)
    up_pre = jnp.dot(flat_in, up_w, preferred_element_type=jnp.float32)
    activated = (jax.nn.silu(gate_pre) * up_pre).astype(jnp.bfloat16)
    partial_out = contract_cols(activated, down_w).reshape(owners, item_count, D)
    returned = lax.all_to_all(
        partial_out.astype(jnp.bfloat16), "expert", split_axis=0, concat_axis=0, tiled=True
    ).astype(partial_out.dtype)
    returned, received, gate_kept, up_kept = (
        returned,
        received,
        gate_pre.reshape(owners, item_count, width_local),
        up_pre.reshape(owners, item_count, width_local),
    )
    slot_out = jnp.sum(returned.reshape(EXPERTS, copies, capacity, D), axis=1).reshape(
        EXPERTS * capacity, D
    )
    expert_rows = jnp.where(
        is_expert[:, None], jnp.take(slot_out, take_index, axis=0), 0.0
    ).reshape(pair_count, 2, D)

    def mixer(normed, normed_low, router_in, proj_in, vec_in, residual_logits, rows_in):
        return mix_part(
            picked, normed, normed_low, router_in, proj_in, vec_in, residual_logits, rows_in
        )

    mixture, mix_back = jax.vjp(
        mixer,
        normed_two,
        normed_two_low.astype(jnp.float32),
        router_f,
        proj_f,
        vec_f,
        gate_residual.reshape(pair_count, EXPERTS + 4),
        expert_rows,
    )
    output = (hidden + mixture).astype(jnp.bfloat16).reshape(row_count, 2, D)
    grad_out = cotangent.reshape(pair_count, D).astype(jnp.float32)
    grad_normed, grad_normed_low, grad_router, grad_proj, grad_vec, grad_logits, grad_rows = (
        mix_back(grad_out)
    )
    grad_assign = grad_rows.reshape(2 * pair_count, D).astype(jnp.bfloat16)
    grad_send = jnp.dot(placement, grad_assign, preferred_element_type=jnp.float32).astype(
        jnp.bfloat16
    )
    grad_got = lax.all_to_all(
        to_owners(grad_send), "expert", split_axis=0, concat_axis=0, tiled=True
    )
    grad_expert = grad_got.reshape(owners * capacity, D)
    flat_in = received.reshape(owners * capacity, D)
    gate_pre = gate_kept.reshape(owners * capacity, width_local)
    up_pre = up_kept.reshape(owners * capacity, width_local)
    sigmoid_gate = jax.nn.sigmoid(gate_pre)
    silu_gate = jax.nn.silu(gate_pre)
    activated = (silu_gate * up_pre).astype(jnp.bfloat16)
    grad_down = contract_rows(grad_expert, activated)
    grad_activated = jnp.dot(grad_expert, down_w, preferred_element_type=jnp.float32)
    grad_gate_pre = (
        grad_activated * up_pre * sigmoid_gate * (1.0 + gate_pre * (1.0 - sigmoid_gate))
    ).astype(jnp.bfloat16)
    grad_up_pre = (grad_activated * silu_gate).astype(jnp.bfloat16)
    grad_owner_in = contract_cols(grad_gate_pre, gate_w) + contract_cols(grad_up_pre, up_w)
    grad_gate_w = contract_rows(flat_in, grad_gate_pre)
    grad_up_w = contract_rows(flat_in, grad_up_pre)
    grad_returned = lax.all_to_all(
        grad_owner_in.reshape(owners, capacity, D).astype(jnp.bfloat16),
        "expert",
        split_axis=0,
        concat_axis=0,
        tiled=True,
    ).astype(jnp.float32)
    grad_slots = jnp.sum(grad_returned.reshape(EXPERTS, copies, capacity, D), axis=1).reshape(
        EXPERTS * capacity, D
    )
    grad_from_experts = jnp.sum(
        jnp.where(is_expert[:, None], jnp.take(grad_slots, take_index, axis=0), 0.0).reshape(
            pair_count, 2, D
        ),
        axis=1,
    )
    expert_grads = (
        lax.psum_scatter(
            grad_gate_w.astype(jnp.bfloat16), "dp", scatter_dimension=0, tiled=True
        ).astype(jnp.float32),
        lax.psum_scatter(
            grad_up_w.astype(jnp.bfloat16), "dp", scatter_dimension=0, tiled=True
        ).astype(jnp.float32),
        lax.psum_scatter(
            grad_down.astype(jnp.bfloat16), "dp", scatter_dimension=0, tiled=True
        ).astype(jnp.float32),
    )
    _, norm_two_back = jax.vjp(rms_scale, hidden, gain_two)
    grad_hidden_norm, grad_gain_two = norm_two_back(
        grad_normed + grad_normed_low + grad_from_experts
    )
    grad_hidden = grad_out + grad_hidden_norm
    grad_branch = grad_hidden.astype(jnp.bfloat16)
    grad_out_w = contract_rows(attended_low, grad_branch)
    attended_gradient = (
        contract_cols(grad_branch, out_w).astype(jnp.bfloat16).reshape(pair_count, HEADS, HEAD_DIM)
    )
    delta = jnp.transpose(jnp.sum(attended_gradient.astype(jnp.float32) * attended, axis=-1))
    kv_back = lax.all_gather(kv_local, "expert", axis=0, tiled=True)
    all_rows = kv_back.shape[0]
    local_step_rows = math.gcd(all_rows, 256)
    key_blocks = kv_back.reshape(all_rows // local_step_rows, local_step_rows, 4 * D)
    offsets = jnp.arange(all_rows // local_step_rows, dtype=jnp.int32) * local_step_rows
    empty_width = 4 * D

    def local_one_block(grad_query, element):
        key_block, offset = element
        seen_mask = visible(own_info, key_side_info(0, offset, local_step_rows))

        def local_compute(grad_query):
            key_value_heads = key_block.reshape(2 * local_step_rows, 2, HEADS, HEAD_DIM)
            score_matrix = (
                jnp.einsum(
                    "stc,atc->tsa",
                    query_matrix,
                    key_value_heads[:, 0],
                    preferred_element_type=jnp.float32,
                )
                * query_key_scale
            )
            weight_matrix = jnp.where(
                seen_mask[None], jnp.exp(score_matrix - log_total[:, :, None]), 0.0
            )
            grad_weights = jnp.einsum(
                "stc,atc->tsa",
                attended_gradient,
                key_value_heads[:, 1],
                preferred_element_type=jnp.float32,
            )
            score_gradient = (weight_matrix * (grad_weights - delta[:, :, None])).astype(
                jnp.bfloat16
            )
            grad_query = grad_query + jnp.einsum(
                "ezt,teu->zeu",
                score_gradient,
                key_value_heads[:, 0],
                preferred_element_type=jnp.float32,
            )
            grad_key = jnp.einsum(
                "sba,bsx->asx", score_gradient, query_matrix, preferred_element_type=jnp.float32
            )
            grad_value = jnp.einsum(
                "sba,bsx->asx",
                weight_matrix.astype(jnp.bfloat16),
                attended_gradient,
                preferred_element_type=jnp.float32,
            )
            grad_block = jnp.concatenate(
                [
                    grad_key.reshape(2 * local_step_rows, D),
                    grad_value.reshape(2 * local_step_rows, D),
                ],
                axis=1,
            ).reshape(local_step_rows, 4 * D)
            return (grad_query, grad_block)

        def skip(grad_query):
            return (grad_query, jnp.zeros((local_step_rows, empty_width), jnp.float32))

        return lax.cond(jnp.any(seen_mask), local_compute, skip, grad_query)

    grad_query, grad_blocks = lax.scan(
        local_one_block,
        jnp.zeros((pair_count, HEADS, HEAD_DIM), jnp.float32),
        (key_blocks, offsets),
    )
    grad_query, grad_whole = (grad_query, grad_blocks.reshape(all_rows, empty_width))
    grad_kv = (
        lax.psum_scatter(grad_whole.astype(jnp.bfloat16), "expert", scatter_dimension=0, tiled=True)
        .astype(jnp.float32)
        .reshape(pair_count, 2, HEADS, HEAD_DIM)
    )
    grad_key = grad_kv[:, 0] * query_key_scale
    grad_value = grad_kv[:, 1]
    grad_query_raw = rotate(grad_query * query_key_scale, -position)
    grad_key_raw = rotate(grad_key, -position)
    grad_qkv = jnp.concatenate(
        [
            grad_query_raw.reshape(pair_count, D),
            grad_key_raw.reshape(pair_count, D),
            grad_value.reshape(pair_count, D),
        ],
        axis=1,
    ).astype(jnp.bfloat16)
    grad_qkv_w = contract_rows(normed_one_low, grad_qkv)
    grad_normed_one = contract_cols(grad_qkv, qkv_w)
    _, norm_one_back = jax.vjp(rms_scale, x_flat, gain_one)
    grad_x_norm, grad_gain_one = norm_one_back(grad_normed_one)
    grad_input = (grad_hidden + grad_x_norm).reshape(row_count, 2, D)
    dense_grads = (
        lax.psum_scatter(grad_gain_one, ("dp", "expert"), scatter_dimension=0, tiled=True),
        lax.psum_scatter(grad_qkv_w, ("dp", "expert"), scatter_dimension=0, tiled=True),
        lax.psum_scatter(grad_out_w, ("dp", "expert"), scatter_dimension=0, tiled=True),
        lax.psum_scatter(grad_gain_two, ("dp", "expert"), scatter_dimension=0, tiled=True),
        lax.psum_scatter(grad_router, ("dp", "expert"), scatter_dimension=0, tiled=True),
        lax.psum_scatter(grad_proj, ("dp", "expert"), scatter_dimension=0, tiled=True),
        lax.psum_scatter(grad_vec, ("dp", "expert"), scatter_dimension=0, tiled=True),
    )
    return (
        output,
        grad_input,
        grad_logits.reshape(row_count, 2, EXPERTS + 4),
        dense_grads[0],
        dense_grads[1],
        dense_grads[2],
        dense_grads[3],
        dense_grads[4],
        dense_grads[5],
        dense_grads[6],
        expert_grads[0],
        expert_grads[1],
        expert_grads[2],
    )


def solution(mesh):
    in_specs = (
        P(("dp", "expert"), None, None),
        P(("dp", "expert"), None, None),
        P(("dp", "expert"), None, None),
        P(("dp", "expert"), None, None),
        P("dp"),
        P("dp"),
        P(("dp", "expert")),
        P(("dp", "expert"), None),
        P(("dp", "expert"), None),
        P(("dp", "expert")),
        P(("dp", "expert"), None),
        P(("dp", "expert"), None),
        P(("dp", "expert"), None),
        P("dp", "expert"),
        P("dp", "expert"),
        P("dp", "expert"),
    )
    out_specs = (
        P(("dp", "expert"), None, None),
        P(("dp", "expert"), None, None),
        P(("dp", "expert"), None, None),
        P(("dp", "expert")),
        P(("dp", "expert"), None),
        P(("dp", "expert"), None),
        P(("dp", "expert")),
        P(("dp", "expert"), None),
        P(("dp", "expert"), None),
        P(("dp", "expert"), None),
        P("dp", "expert"),
        P("dp", "expert"),
        P("dp", "expert"),
    )
    return jax.shard_map(
        per_device, mesh=mesh, in_specs=in_specs, out_specs=out_specs, check_vma=False
    )
```

profile of v0, /device:TPU:0, one launch (start us, length us, event | category | flops | bytes accessed | tf_op | source)
XLA Modules:
  0.0 2076.2 jit_solution(17965394610821876164)
XLA Ops:
  12.2 42.2 %all-reduce.12 = (bf16[768]{0:T(1024)(128)(2,1)S(1)}, bf16[768]{0:T(1024)(128)(2,1)}) all-reduce(bf16[768]{0:T(1024)(128)(2,1)S(1)} %dynamic-update-slice, bf16[768]{0:T(1024)(128)(2,1)S(1)} %dynamic-update-slice.1), channel_id=1, replica_groups=mesh['dp'=4,'expert'=8] {'dp','expert'}, use_global_device_ids=true, to_apply=%add.4 | all-reduce | flops 1536 | bytes 6144
  56.8 16.9 all-gather.10.cloned.1.call-done
  95.4 167.0 %all-gather.12.cloned.1.call-done = bf16[2048,3072]{1,0:T(8,128)(2,1)} async-done(((bf16[256,3072]{1,0:T(8,128)(2,1)}), bf16[2048,3072]{1,0:T(8,128)(2,1)}) %all-gather.12.cloned.1.call-update) | async-done | bytes 12582928 | tf_op jit(solution)/shard_map/all_gather | solution.py:180
  263.7 308.7 %while.41 = (s32[]{:T(128)}, f32[12,512]{1,0:T(8,128)S(1)}, f32[12,512]{1,0:T(8,128)S(1)}, f32[12,512,64]{1,2,0:T(8,128)}, s32[8]{0:T(128)}, /*index=5*/s32[512]...) while((s32[]{:T(128)}, f32[12,512]{1,0:T(8,128)S(1)}, ...), condition=%wide.region_9.10_spmd.clone.clone.clone, body=%wide.region_2.9_spmd.clone.clone.clone.sunk | while | flops 850986752 | bytes 107663672 | solution.py:220
  268.6 33.6 %conditional.10 = ((f32[12,512]{1,0:T(8,128)S(1)}, f32[12,512]{1,0:T(8,128)S(1)}, f32[12,512,64]{1,2,0:T(8,128)})) conditional(s32[]{:T(128)} %convert_element_type.244, (f32[12,512]{1,0:T(8,128)S(1)}, f32[12,512]{1,0:T(8,128)S(1)}, f32[12,512,64]{1,2,0:T(8,128)}) %tuple.197, (pred[512,512]{0,1:T(8,128)(4,1)S(1)}, bf16[8,256,3072]{2,1,0:T(8,128)(2,1)}, ...), branch_computations={%region_5.5_spmd, %region_6.8_spmd} | conditional | flops 846999552 | bytes 107348032 | solution.py:218
  307.1 34.0 %conditional.10 = ((f32[12,512]{1,0:T(8,128)S(1)}, f32[12,512]{1,0:T(8,128)S(1)}, f32[12,512,64]{1,2,0:T(8,128)})) conditional(s32[]{:T(128)} %convert_element_type.244, (f32[12,512]{1,0:T(8,128)S(1)}, f32[12,512]{1,0:T(8,128)S(1)}, f32[12,512,64]{1,2,0:T(8,128)}) %tuple.197, (pred[512,512]{0,1:T(8,128)(4,1)S(1)}, bf16[8,256,3072]{2,1,0:T(8,128)(2,1)}, ...), branch_computations={%region_5.5_spmd, %region_6.8_spmd} | conditional | flops 846999552 | bytes 107348032 | solution.py:218
  346.0 33.9 %conditional.10 = ((f32[12,512]{1,0:T(8,128)S(1)}, f32[12,512]{1,0:T(8,128)S(1)}, f32[12,512,64]{1,2,0:T(8,128)})) conditional(s32[]{:T(128)} %convert_element_type.244, (f32[12,512]{1,0:T(8,128)S(1)}, f32[12,512]{1,0:T(8,128)S(1)}, f32[12,512,64]{1,2,0:T(8,128)}) %tuple.197, (pred[512,512]{0,1:T(8,128)(4,1)S(1)}, bf16[8,256,3072]{2,1,0:T(8,128)(2,1)}, ...), branch_computations={%region_5.5_spmd, %region_6.8_spmd} | conditional | flops 846999552 | bytes 107348032 | solution.py:218
  384.8 33.5 %conditional.10 = ((f32[12,512]{1,0:T(8,128)S(1)}, f32[12,512]{1,0:T(8,128)S(1)}, f32[12,512,64]{1,2,0:T(8,128)})) conditional(s32[]{:T(128)} %convert_element_type.244, (f32[12,512]{1,0:T(8,128)S(1)}, f32[12,512]{1,0:T(8,128)S(1)}, f32[12,512,64]{1,2,0:T(8,128)}) %tuple.197, (pred[512,512]{0,1:T(8,128)(4,1)S(1)}, bf16[8,256,3072]{2,1,0:T(8,128)(2,1)}, ...), branch_computations={%region_5.5_spmd, %region_6.8_spmd} | conditional | flops 846999552 | bytes 107348032 | solution.py:218
  423.3 33.5 %conditional.10 = ((f32[12,512]{1,0:T(8,128)S(1)}, f32[12,512]{1,0:T(8,128)S(1)}, f32[12,512,64]{1,2,0:T(8,128)})) conditional(s32[]{:T(128)} %convert_element_type.244, (f32[12,512]{1,0:T(8,128)S(1)}, f32[12,512]{1,0:T(8,128)S(1)}, f32[12,512,64]{1,2,0:T(8,128)}) %tuple.197, (pred[512,512]{0,1:T(8,128)(4,1)S(1)}, bf16[8,256,3072]{2,1,0:T(8,128)(2,1)}, ...), branch_computations={%region_5.5_spmd, %region_6.8_spmd} | conditional | flops 846999552 | bytes 107348032 | solution.py:218
  461.8 33.5 %conditional.10 = ((f32[12,512]{1,0:T(8,128)S(1)}, f32[12,512]{1,0:T(8,128)S(1)}, f32[12,512,64]{1,2,0:T(8,128)})) conditional(s32[]{:T(128)} %convert_element_type.244, (f32[12,512]{1,0:T(8,128)S(1)}, f32[12,512]{1,0:T(8,128)S(1)}, f32[12,512,64]{1,2,0:T(8,128)}) %tuple.197, (pred[512,512]{0,1:T(8,128)(4,1)S(1)}, bf16[8,256,3072]{2,1,0:T(8,128)(2,1)}, ...), branch_computations={%region_5.5_spmd, %region_6.8_spmd} | conditional | flops 846999552 | bytes 107348032 | solution.py:218
  500.2 33.5 %conditional.10 = ((f32[12,512]{1,0:T(8,128)S(1)}, f32[12,512]{1,0:T(8,128)S(1)}, f32[12,512,64]{1,2,0:T(8,128)})) conditional(s32[]{:T(128)} %convert_element_type.244, (f32[12,512]{1,0:T(8,128)S(1)}, f32[12,512]{1,0:T(8,128)S(1)}, f32[12,512,64]{1,2,0:T(8,128)}) %tuple.197, (pred[512,512]{0,1:T(8,128)(4,1)S(1)}, bf16[8,256,3072]{2,1,0:T(8,128)(2,1)}, ...), branch_computations={%region_5.5_spmd, %region_6.8_spmd} | conditional | flops 846999552 | bytes 107348032 | solution.py:218
  538.7 33.5 %conditional.10 = ((f32[12,512]{1,0:T(8,128)S(1)}, f32[12,512]{1,0:T(8,128)S(1)}, f32[12,512,64]{1,2,0:T(8,128)})) conditional(s32[]{:T(128)} %convert_element_type.244, (f32[12,512]{1,0:T(8,128)S(1)}, f32[12,512]{1,0:T(8,128)S(1)}, f32[12,512,64]{1,2,0:T(8,128)}) %tuple.197, (pred[512,512]{0,1:T(8,128)(4,1)S(1)}, bf16[8,256,3072]{2,1,0:T(8,128)(2,1)}, ...), branch_computations={%region_5.5_spmd, %region_6.8_spmd} | conditional | flops 846999552 | bytes 107348032 | solution.py:218
  600.3 82.8 %all-gather.2 = bf16[32,24,2]{1,2,0:T(2,128)(2,1)S(1)} all-gather(bf16[1,24,2]{1,2,0:T(2,128)(2,1)S(1)} %bitcast.207), channel_id=1, replica_groups=mesh['dp'=4,'expert'=8] {'dp','expert'}, dimensions={0}, use_global_device_ids=true | all-gather | bytes 3168 | tf_op jit(solution)/shard_map/all_gather | solution.py:130
  683.4 63.5 %all-gather.1 = bf16[32,24,4]{1,2,0:T(4,128)(2,1)S(1)} all-gather(bf16[1,24,4]{1,2,0:T(4,128)(2,1)S(1)} %bitcast.206), channel_id=1, replica_groups=mesh['dp'=4,'expert'=8] {'dp','expert'}, dimensions={0}, use_global_device_ids=true | all-gather | bytes 6336 | tf_op jit(solution)/shard_map/all_gather | solution.py:129
  748.7 66.5 %all-gather = bf16[32,24,12]{1,2,0:T(8,128)(2,1)S(1)} all-gather(bf16[1,24,12]{1,2,0:T(8,128)(2,1)S(1)} %bitcast.205), channel_id=1, replica_groups=mesh['dp'=4,'expert'=8] {'dp','expert'}, dimensions={0}, use_global_device_ids=true | all-gather | bytes 19008 | tf_op jit(solution)/shard_map/all_gather | solution.py:128
  922.0 15.1 fusion.58
  978.4 24.1 %multiply_reduce_fusion = (f32[2,768]{1,0:T(2,128)}, f32[512,2]{1,0:T(8,128)S(1)}, f32[512,2]{1,0:T(8,128)S(1)}, f32[512,768]{1,0:T(8,128)}, f32[512,768]{1,0:T(8,128)}) fusion(f32[512,2]{1,0:T(8,128)} %copy-done.38, f32[512,1,768]{2,1,0:T(1,128)} %broadcast_in_dim.334, f32[512,1,768]{2,1,0:T(1,128)} %broadcast_in_dim.333, f32[2,768]{1,0:T(2,128)S(1)} %bitcast.201, ...), kind=kLoop, calls=%fused_computation.138 | loop fusion | flops 12579328 | bytes 14191616 | tf_op jit(solution)/shard_map/transpose(jvp())/reduce_sum | solution.py:77
  1043.8 469.3 %while.42 = (s32[]{:T(128)}, f32[512,12,64]{0,2,1:T(8,128)}, bf16[8,256,3072]{2,1,0:T(8,128)(2,1)}, s32[8]{0:T(128)}, s32[512]{0:T(512)S(1)}, /*index=5*/s32[8]{...) while((s32[]{:T(128)}, f32[512,12,64]{0,2,1:T(8,128)}, ...), condition=%wide.region_38.40_spmd.clone.clone.clone, body=%wide.region_33.39_spmd.clone.clone.clone.sunk | while | flops 2052249344 | bytes 105509768 | solution.py:417
  1049.8 50.0 %conditional.11 = (f32[512,12,64]{0,2,1:T(8,128)}, bf16[1,256,3072]{2,1,0:T(8,128)(2,1)}) conditional(s32[]{:T(128)} %convert_element_type.245, f32[512,12,64]{0,2,1:T(8,128)} %get-tuple-element.1261, (pred[512,512]{0,1:T(8,128)(4,1)S(1)}, bf16[8,256,3072]{2,1,0:T(8,128)(2,1)}, s32[]{:T(128)}, bf16[512,12,64]{0,2,1:T(8,128)(2,1)S(1)}, ...), branch_computations={%region_36.37_spmd, %region_37.38_spmd} | conditional | flops 2048262144 | bytes 95756368 | solution.py:415
  1108.4 50.0 %conditional.11 = (f32[512,12,64]{0,2,1:T(8,128)}, bf16[1,256,3072]{2,1,0:T(8,128)(2,1)}) conditional(s32[]{:T(128)} %convert_element_type.245, f32[512,12,64]{0,2,1:T(8,128)} %get-tuple-element.1261, (pred[512,512]{0,1:T(8,128)(4,1)S(1)}, bf16[8,256,3072]{2,1,0:T(8,128)(2,1)}, s32[]{:T(128)}, bf16[512,12,64]{0,2,1:T(8,128)(2,1)S(1)}, ...), branch_computations={%region_36.37_spmd, %region_37.38_spmd} | conditional | flops 2048262144 | bytes 95756368 | solution.py:415
  1167.0 50.0 %conditional.11 = (f32[512,12,64]{0,2,1:T(8,128)}, bf16[1,256,3072]{2,1,0:T(8,128)(2,1)}) conditional(s32[]{:T(128)} %convert_element_type.245, f32[512,12,64]{0,2,1:T(8,128)} %get-tuple-element.1261, (pred[512,512]{0,1:T(8,128)(4,1)S(1)}, bf16[8,256,3072]{2,1,0:T(8,128)(2,1)}, s32[]{:T(128)}, bf16[512,12,64]{0,2,1:T(8,128)(2,1)S(1)}, ...), branch_computations={%region_36.37_spmd, %region_37.38_spmd} | conditional | flops 2048262144 | bytes 95756368 | solution.py:415
  1225.5 50.0 %conditional.11 = (f32[512,12,64]{0,2,1:T(8,128)}, bf16[1,256,3072]{2,1,0:T(8,128)(2,1)}) conditional(s32[]{:T(128)} %convert_element_type.245, f32[512,12,64]{0,2,1:T(8,128)} %get-tuple-element.1261, (pred[512,512]{0,1:T(8,128)(4,1)S(1)}, bf16[8,256,3072]{2,1,0:T(8,128)(2,1)}, s32[]{:T(128)}, bf16[512,12,64]{0,2,1:T(8,128)(2,1)S(1)}, ...), branch_computations={%region_36.37_spmd, %region_37.38_spmd} | conditional | flops 2048262144 | bytes 95756368 | solution.py:415
  1284.1 50.0 %conditional.11 = (f32[512,12,64]{0,2,1:T(8,128)}, bf16[1,256,3072]{2,1,0:T(8,128)(2,1)}) conditional(s32[]{:T(128)} %convert_element_type.245, f32[512,12,64]{0,2,1:T(8,128)} %get-tuple-element.1261, (pred[512,512]{0,1:T(8,128)(4,1)S(1)}, bf16[8,256,3072]{2,1,0:T(8,128)(2,1)}, s32[]{:T(128)}, bf16[512,12,64]{0,2,1:T(8,128)(2,1)S(1)}, ...), branch_computations={%region_36.37_spmd, %region_37.38_spmd} | conditional | flops 2048262144 | bytes 95756368 | solution.py:415
  1342.7 50.0 %conditional.11 = (f32[512,12,64]{0,2,1:T(8,128)}, bf16[1,256,3072]{2,1,0:T(8,128)(2,1)}) conditional(s32[]{:T(128)} %convert_element_type.245, f32[512,12,64]{0,2,1:T(8,128)} %get-tuple-element.1261, (pred[512,512]{0,1:T(8,128)(4,1)S(1)}, bf16[8,256,3072]{2,1,0:T(8,128)(2,1)}, s32[]{:T(128)}, bf16[512,12,64]{0,2,1:T(8,128)(2,1)S(1)}, ...), branch_computations={%region_36.37_spmd, %region_37.38_spmd} | conditional | flops 2048262144 | bytes 95756368 | solution.py:415
  1401.3 50.0 %conditional.11 = (f32[512,12,64]{0,2,1:T(8,128)}, bf16[1,256,3072]{2,1,0:T(8,128)(2,1)}) conditional(s32[]{:T(128)} %convert_element_type.245, f32[512,12,64]{0,2,1:T(8,128)} %get-tuple-element.1261, (pred[512,512]{0,1:T(8,128)(4,1)S(1)}, bf16[8,256,3072]{2,1,0:T(8,128)(2,1)}, s32[]{:T(128)}, bf16[512,12,64]{0,2,1:T(8,128)(2,1)S(1)}, ...), branch_computations={%region_36.37_spmd, %region_37.38_spmd} | conditional | flops 2048262144 | bytes 95756368 | solution.py:415
  1459.8 50.0 %conditional.11 = (f32[512,12,64]{0,2,1:T(8,128)}, bf16[1,256,3072]{2,1,0:T(8,128)(2,1)}) conditional(s32[]{:T(128)} %convert_element_type.245, f32[512,12,64]{0,2,1:T(8,128)} %get-tuple-element.1261, (pred[512,512]{0,1:T(8,128)(4,1)S(1)}, bf16[8,256,3072]{2,1,0:T(8,128)(2,1)}, s32[]{:T(128)}, bf16[512,12,64]{0,2,1:T(8,128)(2,1)S(1)}, ...), branch_computations={%region_36.37_spmd, %region_37.38_spmd} | conditional | flops 2048262144 | bytes 95756368 | solution.py:415
  1543.4 175.2 %reduce-scatter.10.cloned.1.call-done = bf16[256,3072]{1,0:T(8,128)(2,1)} async-done(((bf16[2048,3072]{1,0:T(8,128)(2,1)}), bf16[256,3072]{1,0:T(8,128)(2,1)}) %reduce-scatter.10.cloned.1.call-update) | async-done | bytes 1572880 | tf_op jit(solution)/shard_map/reduce_scatter | solution.py:424
  1760.6 38.0 %reduce-scatter.18.cloned.1.call-done = bf16[192,2048]{1,0:T(8,128)(2,1)} async-done(((bf16[768,2048]{1,0:T(8,128)(2,1)}), bf16[192,2048]{1,0:T(8,128)(2,1)}) %reduce-scatter.18.cloned.1.call-update) | async-done | bytes 786448 | tf_op jit(solution)/shard_map/reduce_scatter | solution.py:336
  1801.1 37.8 %reduce-scatter.20.cloned.1.call-done = bf16[192,2048]{1,0:T(8,128)(2,1)} async-done(((bf16[768,2048]{1,0:T(8,128)(2,1)}), bf16[192,2048]{1,0:T(8,128)(2,1)}) %reduce-scatter.20.cloned.1.call-update) | async-done | bytes 786448 | tf_op jit(solution)/shard_map/reduce_scatter | solution.py:339
  1851.2 40.5 %all-reduce.11 = (f32[768]{0:T(1024)S(1)}, f32[768]{0:T(1024)S(1)}, f32[768,12]{0,1:T(8,128)S(1)}, f32[768,4]{0,1:T(4,128)S(1)}, f32[768,2]{0,1:T(2,128)S(1)}) all-reduce(f32[768]{0:T(1024)S(1)} %get-tuple-element.880, f32[768]{0:T(1024)S(1)} %copy-done.85, ...), channel_id=3, replica_groups=mesh['dp'=4,'expert'=8] {'dp','expert'}, use_global_device_ids=true, to_apply=%region_42.44.clone | all-reduce | flops 15360 | bytes 122880
  1894.8 49.7 %reduce-scatter.14.cloned.1.call-done = f32[24,768]{1,0:T(8,128)} async-done(((f32[768,768]{1,0:T(8,128)}), f32[24,768]{1,0:T(8,128)}) %reduce-scatter.14.cloned.1.call-update) | async-done | bytes 73744 | tf_op jit(solution)/shard_map/reduce_scatter | solution.py:448
  1944.5 124.7 %reduce-scatter.12.cloned.1.call-done = f32[24,2304]{1,0:T(8,128)} async-done(((f32[768,2304]{1,0:T(8,128)}), f32[24,2304]{1,0:T(8,128)}) %reduce-scatter.12.cloned.1.call-update) | async-done | bytes 221200 | tf_op jit(solution)/shard_map/reduce_scatter | solution.py:447
  (888 shorter events, 1103.4 us)
Async XLA Ops:
  7.2 47.2 %copy-start.32 = (bf16[256,2,768]{2,1,0:T(2,128)(2,1)S(1)}, bf16[256,2,768]{2,1,0:T(2,128)(2,1)}, u32[]{:S(2)}) copy-start(bf16[256,2,768]{2,1,0:T(2,128)(2,1)} %param.26) | copy-start | bytes 2359300
  7.2 66.6 %all-gather.10.cloned.1.call-start = ((), (), s32[]{:S(2)}) async-start(), calls=%async_computation.10 | async-start | bytes 3649536 | tf_op jit(solution)/shard_map/all_gather | solution.py:125
  7.9 254.5 %all-gather.12.cloned.1.call-start = ((), (), s32[]{:S(2)}) async-start(), calls=%async_computation.11 | async-start | bytes 14155776 | tf_op jit(solution)/shard_map/all_gather | solution.py:180
  10.2 67.7 %copy-start.15 = (f32[512,768]{1,0:T(8,128)}, f32[512,768]{1,0:T(8,128)S(1)}, u32[]{:S(2)}) copy-start(f32[512,768]{1,0:T(8,128)S(1)} %reshape.969) | copy-start | bytes 4718596
  87.4 487.0 %all-gather.14.cloned.1.call-start = ((), (), s32[]{:S(2)}) async-start(), calls=%async_computation.12 | async-start | bytes 1216512 | tf_op jit(solution)/shard_map/all_gather | solution.py:126
  88.1 175.6 %copy-start.66 = (s32[8]{0:T(128)S(1)}, s32[8]{0:T(128)}, u32[]{:S(2)}) copy-start(s32[8]{0:T(128)} %param.31) | copy-start | bytes 100
  88.1 727.8 %all-gather.16.cloned.1.call-start = ((), (), s32[]{:S(2)}) async-start(), calls=%async_computation.13 | async-start | bytes 3932160 | tf_op jit(solution)/shard_map/all_gather | solution.py:140
  88.7 736.3 %all-gather.18.cloned.1.call-start = ((), (), s32[]{:S(2)}) async-start(), calls=%async_computation.14 | async-start | bytes 3932160 | tf_op jit(solution)/shard_map/all_gather | solution.py:141
  579.9 305.8 %copy-start.4 = (bf16[512,768]{1,0:T(8,128)(2,1)}, bf16[512,768]{1,0:T(8,128)(2,1)S(1)}, u32[]{:S(2)}) copy-start(bf16[512,768]{1,0:T(8,128)(2,1)S(1)} %get-tuple-element.956) | copy-start | bytes 2359300
  586.8 229.2 %all-to-all-start = ((bf16[8,128,768]{2,1,0:T(8,128)(2,1)}), bf16[8,128,768]{2,1,0:T(8,128)(2,1)}, u32[]{:S(2)}, u32[]{:S(2)}) async-start(bf16[8,128,768]{2,1,0:T(8,128)(2,1)} %bitcast.22), calls=%async_computation | async-start | bytes 3145728 | tf_op jit(solution)/shard_map/all_to_all | solution.py:248
  591.2 246.8 %all-gather.20.cloned.1.call-start = ((), (), s32[]{:S(2)}) async-start(), calls=%async_computation.15 | async-start | bytes 3932160 | tf_op jit(solution)/shard_map/all_gather | solution.py:142
  594.9 88.5 %copy-start.102 = (bf16[24,4]{0,1:T(4,128)(2,1)S(1)}, bf16[24,4]{0,1:T(4,128)(2,1)}, u32[]{:S(2)}) copy-start(bf16[24,4]{0,1:T(4,128)(2,1)} %param.37) | copy-start | bytes 580
  594.9 152.8 %copy-start.78 = (f32[256,2,12]{0,1,2:T(2,128)S(1)}, f32[256,2,12]{0,1,2:T(2,128)}, u32[]{:S(2)}) copy-start(f32[256,2,12]{0,1,2:T(2,128)} %param.28) | copy-start | bytes 73732
  594.9 153.7 %copy-start.100 = (bf16[24,12]{0,1:T(8,128)(2,1)S(1)}, bf16[24,12]{0,1:T(8,128)(2,1)}, u32[]{:S(2)}) copy-start(bf16[24,12]{0,1:T(8,128)(2,1)} %param.36) | copy-start | bytes 1732
  594.9 220.4 %copy-start.86 = (pred[1024]{0:T(1024)(128)(4,1)S(1)}, pred[1024]{0:T(1024)(128)(4,1)}, u32[]{:S(2)}) copy-start(pred[1024]{0:T(1024)(128)(4,1)} %get-tuple-element.955) | copy-start | bytes 3076
  683.4 168.3 %copy-start.64 = (f32[768,2]{0,1:T(2,128)}, f32[768,2]{0,1:T(2,128)S(1)}, u32[]{:S(2)}) copy-start(f32[768,2]{0,1:T(2,128)S(1)} %reshape.1003) | copy-start | bytes 18436
  815.3 70.4 %copy-start.57 = (bf16[768,12]{0,1:T(8,128)(2,1)}, bf16[768,12]{0,1:T(8,128)(2,1)S(1)}, u32[]{:S(2)}) copy-start(bf16[768,12]{0,1:T(8,128)(2,1)S(1)} %reshape.998) | copy-start | bytes 55300
  845.8 40.9 %all-to-all-start.1 = ((bf16[8,128,768]{2,1,0:T(8,128)(2,1)}), bf16[8,128,768]{2,1,0:T(8,128)(2,1)}, u32[]{:S(2)}, u32[]{:S(2)}) async-start(bf16[8,128,768]{2,1,0:T(8,128)(2,1)} %bitcast.24), calls=%async_computation.1 | async-start | bytes 3145728 | tf_op jit(solution)/shard_map/all_to_all | solution.py:257
  913.2 40.1 %all-to-all-start.2 = ((bf16[8,128,768]{2,1,0:T(8,128)(2,1)}), bf16[8,128,768]{2,1,0:T(8,128)(2,1)}, u32[]{:S(2)}, u32[]{:S(2)}) async-start(bf16[8,128,768]{2,1,0:T(8,128)(2,1)} %bitcast.189), calls=%async_computation.2 | async-start | bytes 3145728 | tf_op jit(solution)/shard_map/all_to_all | solution.py:297
  973.7 40.7 %all-to-all-start.3 = ((bf16[8,128,768]{2,1,0:T(8,128)(2,1)}), bf16[8,128,768]{2,1,0:T(8,128)(2,1)}, u32[]{:S(2)}, u32[]{:S(2)}) async-start(bf16[8,128,768]{2,1,0:T(8,128)(2,1)} %bitcast.188), calls=%async_computation.3 | async-start | bytes 3145728 | tf_op jit(solution)/shard_map/all_to_all | solution.py:316
  978.3 740.3 %reduce-scatter.10.cloned.1.call-start = ((), (), s32[]{:S(2)}) async-start(), calls=%async_computation.16 | async-start | bytes 14155776 | tf_op jit(solution)/shard_map/reduce_scatter | solution.py:424
  978.4 24.2 %copy-start.21 = (f32[512,2,2]{1,0,2:T(8,128)S(1)}, f32[512,2,2]{1,0,2:T(8,128)}, u32[]{:S(2)}) copy-start(f32[512,2,2]{1,0,2:T(8,128)} %copy-done.20) | copy-start | bytes 24580
  978.4 24.2 %copy-start.41 = (f32[512,2]{1,0:T(8,128)S(1)}, f32[512,2]{1,0:T(8,128)}, u32[]{:S(2)}) copy-start(f32[512,2]{1,0:T(8,128)} %multiply_divide_fusion) | copy-start | bytes 12292
  978.4 24.3 %copy-start.30 = (f32[512,2]{1,0:T(8,128)S(1)}, f32[512,2]{1,0:T(8,128)}, u32[]{:S(2)}) copy-start(f32[512,2]{1,0:T(8,128)} %copy-done.28) | copy-start | bytes 12292
  1003.3 29.2 %copy-start.51 = (f32[512,12]{0,1:T(8,128)}, f32[512,12]{0,1:T(8,128)S(1)}, u32[]{:S(2)}) copy-start(f32[512,12]{0,1:T(8,128)S(1)} %add_multiply_fusion.1) | copy-start | bytes 73732
  1513.1 245.1 %reduce-scatter.16.cloned.1.call-start = ((), (), s32[]{:S(2)}) async-start(), calls=%async_computation.19 | async-start | bytes 3932160 | tf_op jit(solution)/shard_map/reduce_scatter | solution.py:333
  1521.1 277.6 %reduce-scatter.18.cloned.1.call-start = ((), (), s32[]{:S(2)}) async-start(), calls=%async_computation.20 | async-start | bytes 3932160 | tf_op jit(solution)/shard_map/reduce_scatter | solution.py:336
  1528.9 310.0 %reduce-scatter.20.cloned.1.call-start = ((), (), s32[]{:S(2)}) async-start(), calls=%async_computation.21 | async-start | bytes 3932160 | tf_op jit(solution)/shard_map/reduce_scatter | solution.py:339
  1536.7 407.8 %reduce-scatter.14.cloned.1.call-start = ((), (), s32[]{:S(2)}) async-start(), calls=%async_computation.18 | async-start | bytes 2433024 | tf_op jit(solution)/shard_map/reduce_scatter | solution.py:448
  1540.6 528.5 %reduce-scatter.12.cloned.1.call-start = ((), (), s32[]{:S(2)}) async-start(), calls=%async_computation.17 | async-start | bytes 7299072 | tf_op jit(solution)/shard_map/reduce_scatter | solution.py:447
  1747.7 93.6 %copy-start.43 = (bf16[512,12,64]{0,2,1:T(8,128)(2,1)S(1)}, bf16[512,12,64]{0,2,1:T(8,128)(2,1)}, u32[]{:S(2)}) copy-start(bf16[512,12,64]{0,2,1:T(8,128)(2,1)} %copy-done.42) | copy-start | bytes 2359300
  1747.7 93.6 %copy-start.45 = (bf16[512,12,64]{0,2,1:T(8,128)(2,1)S(1)}, bf16[512,12,64]{0,2,1:T(8,128)(2,1)}, u32[]{:S(2)}) copy-start(bf16[512,12,64]{0,2,1:T(8,128)(2,1)} %copy-done.44) | copy-start | bytes 2359300
  (128 other events, 661.2 us)
Sparse Core Ops, SparseCore 0:
  10.9 62.8 all-gather.9
  87.5 174.8 all-gather.11
  265.3 52.2 all-gather.13
  319.0 27.3 all-gather.15
  347.8 28.4 all-gather.17
  593.3 29.8 all-gather.19
  1513.2 205.3 reduce-scatter.9
  1721.1 36.9 reduce-scatter.15
  1760.7 37.8 reduce-scatter.17
  1801.0 37.8 reduce-scatter.19
  1844.8 99.6 reduce-scatter.13
  1950.6 118.5 reduce-scatter.11
where the time goes:
time: 2090 us; the launch traced here: 2080 us
  waiting for transfers between devices  640 us (31%)
  local copies, waits for them, and re-layouts  488 us (23%)
  matrix products  443 us (21%)
  blocking collectives  295 us (14%)
  other arithmetic  160 us (8%)
    reduce_scatter x1, waiting for transfers between devices, per_device(): lax.psum_scatter(grad_whole.astype(jnp.bfloat16), 'expert', scatter_dimen...  175 us
    all_gather x1, waiting for transfers between devices, per_device(): piece = lax.all_gather(kv_local, 'expert', axis=0, tiled=True)  167 us
    reduce_scatter x1, waiting for transfers between devices, per_device(): lax.psum_scatter(grad_qkv_w, ('dp', 'expert'), scatter_dimension=0, tiled...  125 us
    cond x88, local copies, waits for them, and re-layouts  97.3 us
    all_gather x1, blocking collectives, per_device(): lax.all_gather(const_vec, ('dp', 'expert'), axis=0, tiled=True)  82.8 us
    unnamed x2, blocking collectives  82.6 us
    dot_general x8, matrix products, fold_compute(): jnp.einsum('rus,srb->rub', weight_matrix.astype(jnp.bfloat16), key_value_...  78.5 us
    dot_general x8, matrix products, local_compute(): jnp.einsum('stc,atc->tsa', attended_gradient, key_value_heads[:, 1], pref...  74.3 us
  transfers between devices with their start and end apart: 16, of which 10 were waited for; matrix products, arithmetic and copies ran while one was open for 25% of the time, Pallas kernels for 0%

commit v1 on v0

v1 whole, which is shorter than its diff:
```python
import functools

import jax
import jax.numpy as jnp
from jax import lax
from jax.experimental import pallas as pl
from jax.experimental.pallas import tpu as pltpu
from jax.sharding import PartitionSpec as P

D = 768
HEADS = 12
HEAD_DIM = 64
PAIRS = 6
EXPERTS = 8
CONT_LEN = 256
PROMPT = 2048
LANES = 128
EPS = 1e-06
NEG = -1e30
LOG2E = 1.4426950408889634
SCALE = float(HEAD_DIM) ** (-0.5)
LC = SCALE * LOG2E
F32 = jnp.float32
BF16 = jnp.bfloat16
ALL_AXES = ("dp", "expert")
VMEM_LIMIT = 60 * 1024 * 1024


def dot(a, b):
    return jnp.dot(a, b, preferred_element_type=F32)


def dot_nt(a, b):
    return lax.dot_general(a, b, (((1,), (1,)), ((), ())), preferred_element_type=F32)


def dot_tn(a, b):
    return lax.dot_general(a, b, (((0,), (0,)), ((), ())), preferred_element_type=F32)


def split_hi_lo(v):
    hi = v.astype(BF16)
    return hi, (v - hi.astype(F32)).astype(BF16)


def params(cost=None):
    return dict(
        compiler_params=pltpu.CompilerParams(vmem_limit_bytes=VMEM_LIMIT),
        cost_estimate=None if cost is None else pl.CostEstimate(
            flops=int(cost[0]), bytes_accessed=int(cost[1]), transcendentals=0
        ),
    )


def shape(dims, dtype):
    return jax.ShapeDtypeStruct(tuple(dims), dtype)


def spec(block, index):
    return pl.BlockSpec(tuple(block), index)


def whole(dims):
    return pl.BlockSpec(tuple(dims), lambda *_: (0,) * len(dims))


SMEM_SPEC = pl.BlockSpec(memory_space=pltpu.SMEM)


def partner(v):
    lane = lax.broadcasted_iota(jnp.int32, v.shape, 1)
    return jnp.where((lane & 63) < 32, pltpu.roll(v, 96, 1), pltpu.roll(v, 32, 1))


def qkv_body(x_ref, gain_ref, wq_ref, wk_ref, wv_ref, c_ref, s_ref, n_ref, q_ref, qt_ref, kv_ref):
    @pl.when(pl.program_id(0) == 0)
    def _():
        x = x_ref[...].astype(F32)
        scale = lax.rsqrt(jnp.mean(x * x, axis=-1, keepdims=True) + EPS)
        n_ref[...] = (x * scale * gain_ref[...]).astype(BF16)

    n = n_ref[...]
    cosine = c_ref[...]
    sine = s_ref[...]
    kv = dot(n, jnp.concatenate([wk_ref[...], wv_ref[...]], axis=1))
    k = kv[:, :LANES]
    kv_ref[:, :LANES] = (k * cosine + partner(k) * sine).astype(BF16)
    kv_ref[:, LANES:] = kv[:, LANES:].astype(BF16)
    q = dot(n, wq_ref[...])
    q = q * cosine + partner(q) * sine
    q_ref[...] = q.astype(BF16)
    qt_ref[...] = q.T.astype(BF16)


def qkv_call(x, gain, pack, cosine, sine):
    t = x.shape[0]
    return pl.pallas_call(
        qkv_body,
        grid=(PAIRS,),
        in_specs=[
            whole((t, D)),
            whole((1, D)),
            spec((D, LANES), lambda i: (0, i)),
            spec((D, LANES), lambda i: (0, PAIRS + i)),
            spec((D, LANES), lambda i: (0, 2 * PAIRS + i)),
            whole((t, LANES)),
            whole((t, LANES)),
        ],
        out_specs=[
            whole((t, D)),
            spec((t, LANES), lambda i: (0, i)),
            spec((LANES, t), lambda i: (i, 0)),
            spec((t, 2 * LANES), lambda i: (0, i)),
        ],
        out_shape=[
            shape((t, D), BF16),
            shape((t, D), BF16),
            shape((D, t), BF16),
            shape((t, 2 * D), BF16),
        ],
        name="qkv_rope",
        **params((2 * t * D * 3 * D, 6 * D * D)),
    )(x, gain, pack, pack, pack, cosine, sine)


def head_rows(v, h):
    row = lax.broadcasted_iota(jnp.int32, v.shape, 0)
    return jnp.where(row // HEAD_DIM == h, v, jnp.zeros_like(v))


def head_lanes(v, h):
    lane = lax.broadcasted_iota(jnp.int32, v.shape, 1)
    return jnp.where(lane // HEAD_DIM == h, v, jnp.zeros_like(v))


def attend_update(qz, kb, vt, lo, hi, mask, st_ref, a_ref, first):
    for h in range(2):
        s = dot(kb, qz[h][:, lo:hi])
        if mask is not None:
            s = jnp.where(mask, s, NEG)
        top = jnp.max(s, axis=0, keepdims=True)
        rows = slice(h * HEAD_DIM, (h + 1) * HEAD_DIM)
        if first:
            p = jnp.exp2((s - top) * LC)
            st_ref[h : h + 1, lo:hi] = top
            st_ref[2 + h : 3 + h, lo:hi] = jnp.sum(p, axis=0, keepdims=True)
            a_ref[rows, lo:hi] = dot(vt[rows], p.astype(BF16))
        else:
            old = st_ref[h : h + 1, lo:hi]
            new = jnp.maximum(old, top)
            alpha = jnp.exp2((old - new) * LC)
            p = jnp.exp2((s - new) * LC)
            st_ref[h : h + 1, lo:hi] = new
            st_ref[2 + h : 3 + h, lo:hi] = st_ref[2 + h : 3 + h, lo:hi] * alpha + jnp.sum(
                p, axis=0, keepdims=True
            )
            a_ref[rows, lo:hi] = a_ref[rows, lo:hi] * alpha + dot(vt[rows], p.astype(BF16))


def local_masks(sc_ref, r, keys, lo, hi):
    cpos = sc_ref[1]
    length = sc_ref[2]
    col = lo + lax.broadcasted_iota(jnp.int32, (r, hi - lo), 1)
    row = lax.broadcasted_iota(jnp.int32, (r, hi - lo), 0)
    own = (row <= col) | (col >= r)
    col = lo + lax.broadcasted_iota(jnp.int32, (keys, hi - lo), 1)
    row = lax.broadcasted_iota(jnp.int32, (keys, hi - lo), 0)
    cont = (col >= r) & (row <= cpos + col - r) & (row < length)
    return own, cont


def fwd_local_body(sc_ref, qt_ref, kv_ref, kvo_ref, st_ref, a_ref):
    t = qt_ref.shape[1]
    r = t // 2
    keys = kvo_ref.shape[0]
    qt = qt_ref[...]
    qz = [head_rows(qt, h) for h in range(2)]
    kb = kv_ref[:, :LANES]
    vt = kv_ref[:, LANES:].T
    kbo = kvo_ref[:, :LANES]
    vto = kvo_ref[:, LANES:].T
    st_ref[...] = jnp.zeros_like(st_ref)
    own, cont = local_masks(sc_ref, r, keys, 0, t)
    if r % LANES == 0:
        attend_update(qz, kb, vt, 0, r, own[:, :r], st_ref, a_ref, True)
        attend_update(qz, kb, vt, r, t, None, st_ref, a_ref, True)
        attend_update(qz, kbo, vto, r, t, cont[:, r:], st_ref, a_ref, False)
    else:
        attend_update(qz, kb, vt, 0, t, own, st_ref, a_ref, True)
        attend_update(qz, kbo, vto, 0, t, cont, st_ref, a_ref, False)


def fwd_remote_body(n, final, sc_ref, qt_ref, kv_ref, st_in, a_in, *outs):
    st_ref, a_ref = outs[0], outs[1]
    t = qt_ref.shape[1]
    r = t // 2
    me = sc_ref[0]
    qt = qt_ref[...]
    qz = [head_rows(qt, h) for h in range(2)]
    st_ref[...] = st_in[...]
    a_ref[...] = a_in[...]
    for j in range(n):
        block = sc_ref[3 + j]
        rows = slice(j * r, (j + 1) * r)

        def go(lo, mask):
            kb = kv_ref[rows, :LANES]
            vt = kv_ref[rows, LANES:].T
            attend_update(qz, kb, vt, lo, t, mask, st_ref, a_ref, False)

        if r % LANES == 0:

            @pl.when(block < me)
            def _():
                go(0, None)

            @pl.when(block > me)
            def _():
                go(r, None)

        else:

            @pl.when(block != me)
            def _():
                col = lax.broadcasted_iota(jnp.int32, (r, t), 1)
                go(0, (col >= r) | (block < me))

    if final:
        low_ref = outs[2]
        for h in range(2):
            rows = slice(h * HEAD_DIM, (h + 1) * HEAD_DIM)
            total = st_ref[2 + h : 3 + h, :]
            a_ref[rows, :] = a_ref[rows, :] / total
            st_ref[h : h + 1, :] = st_ref[h : h + 1, :] * LC + jnp.log2(total)
        low_ref[...] = a_ref[...].T.astype(BF16)


def fwd_local(sc, qt, kv_prompt, kv_own):
    t = qt.shape[1]
    keys = kv_own.shape[0]
    return pl.pallas_call(
        fwd_local_body,
        grid=(PAIRS,),
        in_specs=[
            SMEM_SPEC,
            spec((LANES, t), lambda i: (i, 0)),
            spec((t // 2, 2 * LANES), lambda i: (0, i)),
            spec((keys, 2 * LANES), lambda i: (0, i)),
        ],
        out_specs=[spec((8, t), lambda i: (i, 0)), spec((LANES, t), lambda i: (i, 0))],
        out_shape=[shape((8 * PAIRS, t), F32), shape((D, t), F32)],
        name="attend_local",
        **params((4 * 4 * t * keys * D, 4 * D * t)),
    )(sc, qt, kv_prompt, kv_own)


def fwd_remote(sc, qt, kv, st, acc, final):
    t = qt.shape[1]
    rows = kv.shape[0]
    out_specs = [spec((8, t), lambda i: (i, 0)), spec((LANES, t), lambda i: (i, 0))]
    out_shape = [shape((8 * PAIRS, t), F32), shape((D, t), F32)]
    if final:
        out_specs.append(spec((t, LANES), lambda i: (0, i)))
        out_shape.append(shape((t, D), BF16))
    return pl.pallas_call(
        functools.partial(fwd_remote_body, rows // (t // 2), final),
        grid=(PAIRS,),
        in_specs=[
            SMEM_SPEC,
            spec((LANES, t), lambda i: (i, 0)),
            spec((rows, 2 * LANES), lambda i: (0, i)),
            spec((8, t), lambda i: (i, 0)),
            spec((LANES, t), lambda i: (i, 0)),
        ],
        out_specs=out_specs,
        out_shape=out_shape,
        name="attend_remote",
        **params((4 * 4 * t * rows * D, 8 * D * t + 4 * D * rows)),
    )(sc, qt, kv, st, acc)


def back_block(ops, kb, vb, kt, lo, hi, mask, dq_ref):
    qz, qn, doz, don, lse, delta = ops
    dk = None
    dv = None
    for h in range(2):
        s = dot(kb, qz[h][:, lo:hi])
        dp = dot(vb, doz[h][:, lo:hi])
        p = jnp.exp2(s * LC - lse[h][:, lo:hi])
        if mask is not None:
            p = jnp.where(mask, p, 0.0)
        ds = (p * (dp - delta[h][:, lo:hi])).astype(BF16)
        dv_h = dot(p.astype(BF16), don[h][lo:hi])
        dk_h = dot(ds, qn[h][lo:hi])
        rows = slice(h * HEAD_DIM, (h + 1) * HEAD_DIM)
        dq_ref[rows, lo:hi] += dot(kt[rows], ds)
        dv = dv_h if dv is None else dv + dv_h
        dk = dk_h if dk is None else dk + dk_h
    return dk, dv


def back_operands(qt_ref, q_ref, dot_ref, do_ref, st_ref):
    qt, q, do_t, do = qt_ref[...], q_ref[...], dot_ref[...], do_ref[...]
    return (
        [head_rows(qt, h) for h in range(2)],
        [head_lanes(q, h) for h in range(2)],
        [head_rows(do_t, h) for h in range(2)],
        [head_lanes(do, h) for h in range(2)],
        [st_ref[h : h + 1, :] for h in range(2)],
        [st_ref[4 + h : 5 + h, :] for h in range(2)],
    )


def bwd_local_body(
    sc_ref, qt_ref, q_ref, dot_ref, do_ref, st_in, a_ref, kv_ref, kvo_ref,
    st_ref, dq_ref, dkv_ref, dkvo_ref,
):
    t = qt_ref.shape[1]
    r = t // 2
    keys = kvo_ref.shape[0]
    st_ref[...] = st_in[...]
    prod = a_ref[...] * dot_ref[...].astype(F32)
    for h in range(2):
        st_ref[4 + h : 5 + h, :] = jnp.sum(
            prod[h * HEAD_DIM : (h + 1) * HEAD_DIM], axis=0, keepdims=True
        )
    ops = back_operands(qt_ref, q_ref, dot_ref, do_ref, st_ref)
    dq_ref[...] = jnp.zeros_like(dq_ref)
    kb, vb = kv_ref[:, :LANES], kv_ref[:, LANES:]
    kbo, vbo = kvo_ref[:, :LANES], kvo_ref[:, LANES:]
    kt, kto = kb.T, kbo.T
    own, cont = local_masks(sc_ref, r, keys, 0, t)
    if r % LANES == 0:
        dk, dv = back_block(ops, kb, vb, kt, 0, r, own[:, :r], dq_ref)
        dk2, dv2 = back_block(ops, kb, vb, kt, r, t, None, dq_ref)
        dk, dv = dk + dk2, dv + dv2
        dko, dvo = back_block(ops, kbo, vbo, kto, r, t, cont[:, r:], dq_ref)
    else:
        dk, dv = back_block(ops, kb, vb, kt, 0, t, own, dq_ref)
        dko, dvo = back_block(ops, kbo, vbo, kto, 0, t, cont, dq_ref)
    dkv_ref[:, :LANES] = dk * SCALE
    dkv_ref[:, LANES:] = dv
    dkvo_ref[:, :LANES] = dko * SCALE
    dkvo_ref[:, LANES:] = dvo


def bwd_remote_body(
    n, final, sc_ref, qt_ref, q_ref, dot_ref, do_ref, st_ref, dq_in, kv_ref, dq_ref, dkv_ref, *outs
):
    t = qt_ref.shape[1]
    r = t // 2
    me = sc_ref[0]
    ops = back_operands(qt_ref, q_ref, dot_ref, do_ref, st_ref)
    dq_ref[...] = dq_in[...]
    for j in range(n):
        block = sc_ref[3 + j]
        rows = slice(j * r, (j + 1) * r)

        def go(lo, mask):
            kb, vb = kv_ref[rows, :LANES], kv_ref[rows, LANES:]
            dk, dv = back_block(ops, kb, vb, kb.T, lo, t, mask, dq_ref)
            dkv_ref[rows, :LANES] = (dk * SCALE).astype(BF16)
            dkv_ref[rows, LANES:] = dv.astype(BF16)

        @pl.when(block == me)
        def _():
            dkv_ref[rows, :] = jnp.zeros((r, 2 * LANES), BF16)

        if r % LANES == 0:

            @pl.when(block < me)
            def _():
                go(0, None)

            @pl.when(block > me)
            def _():
                go(r, None)

        else:

            @pl.when(block != me)
            def _():
                col = lax.broadcasted_iota(jnp.int32, (r, t), 1)
                go(0, (col >= r) | (block < me))

    if final:
        outs[0][...] = dq_ref[...].T * SCALE


def q_specs(t):
    return [
        spec((LANES, t), lambda i: (i, 0)),
        spec((t, LANES), lambda i: (0, i)),
        spec((LANES, t), lambda i: (i, 0)),
        spec((t, LANES), lambda i: (0, i)),
        spec((8, t), lambda i: (i, 0)),
    ]


def bwd_local(sc, qt, q, do_t, do, st, att_t, kv_prompt, kv_own):
    t = qt.shape[1]
    keys = kv_own.shape[0]
    return pl.pallas_call(
        bwd_local_body,
        grid=(PAIRS,),
        in_specs=[SMEM_SPEC]
        + q_specs(t)
        + [
            spec((LANES, t), lambda i: (i, 0)),
            spec((t // 2, 2 * LANES), lambda i: (0, i)),
            spec((keys, 2 * LANES), lambda i: (0, i)),
        ],
        out_specs=[
            spec((8, t), lambda i: (i, 0)),
            spec((LANES, t), lambda i: (i, 0)),
            spec((t // 2, 2 * LANES), lambda i: (0, i)),
            spec((keys, 2 * LANES), lambda i: (0, i)),
        ],
        out_shape=[
            shape((8 * PAIRS, t), F32),
            shape((D, t), F32),
            shape((t // 2, 2 * D), F32),
            shape((keys, 2 * D), F32),
        ],
        name="attend_back_local",
        **params((10 * 4 * t * keys * D, 16 * D * t)),
    )(sc, qt, q, do_t, do, st, att_t, kv_prompt, kv_own)


def bwd_remote(sc, qt, q, do_t, do, st, dq, kv, final):
    t = qt.shape[1]
    rows = kv.shape[0]
    out_specs = [spec((LANES, t), lambda i: (i, 0)), spec((rows, 2 * LANES), lambda i: (0, i))]
    out_shape = [shape((D, t), F32), shape((rows, 2 * D), BF16)]
    if final:
        out_specs.append(spec((t, LANES), lambda i: (0, i)))
        out_shape.append(shape((t, D), F32))
    return pl.pallas_call(
        functools.partial(bwd_remote_body, rows // (t // 2), final),
        grid=(PAIRS,),
        in_specs=[SMEM_SPEC]
        + q_specs(t)
        + [spec((LANES, t), lambda i: (i, 0)), spec((rows, 2 * LANES), lambda i: (0, i))],
        out_specs=out_specs,
        out_shape=out_shape,
        name="attend_back_remote",
        **params((10 * 4 * t * rows * D, 16 * D * t + 8 * D * rows)),
    )(sc, qt, q, do_t, do, st, dq, kv)


def route_body(
    x_ref, att_ref, ow_ref, sw_ref, gain_ref, res_ref, rt_ref, tc_ref, tr_ref,
    h_ref, n_ref, pr_ref, xs_ref, ms_ref,
):
    t = x_ref.shape[0]
    step = pl.program_id(0)

    @pl.when(step == 0)
    def _():
        hidden = x_ref[...].astype(F32) + dot(att_ref[...], ow_ref[...])
        h_ref[...] = hidden
        scale = lax.rsqrt(jnp.mean(hidden * hidden, axis=-1, keepdims=True) + EPS)
        low = (hidden * scale * gain_ref[...]).astype(BF16)
        n_ref[...] = low
        z = dot(low, sw_ref[...])
        lane = lax.broadcasted_iota(jnp.int32, (t, LANES), 1)
        is_route = lane < EXPERTS + 4
        logits = jnp.where(is_route, z + res_ref[...], NEG)
        ex = jnp.exp(logits - jnp.max(logits, axis=-1, keepdims=True))
        probs = ex / jnp.sum(ex, axis=-1, keepdims=True)
        out = probs
        first = EXPERTS + 4
        for k in range(2):
            l0 = z[:, first + 2 * k : first + 2 * k + 1]
            l1 = z[:, first + 2 * k + 1 : first + 2 * k + 2]
            top = jnp.maximum(l0, l1)
            e0 = jnp.exp(l0 - top)
            e1 = jnp.exp(l1 - top)
            den = e0 + e1
            out = jnp.where(lane == first + 2 * k, e0 / den, out)
            out = jnp.where(lane == first + 2 * k + 1, e1 / den, out)
        for j in range(2):
            mix = jnp.sum(jnp.where(lane == rt_ref[:, j : j + 1], probs, 0.0), axis=-1, keepdims=True)
            out = jnp.where(lane == 16 + j, mix, out)
        pr_ref[...] = out

    slots = xs_ref.shape[0]
    base = step * slots
    slot = base + lax.broadcasted_iota(jnp.int32, (slots, t), 0)
    pick = (slot == tr_ref[0:1, :]) | (slot == tr_ref[1:2, :])
    xs_ref[...] = dot(pick.astype(BF16), n_ref[...]).astype(BF16)
    slot = base + lax.broadcasted_iota(jnp.int32, (t, slots), 1)
    mixes = jnp.where(slot == tc_ref[:, 0:1], pr_ref[:, 16:17], 0.0) + jnp.where(
        slot == tc_ref[:, 1:2], pr_ref[:, 17:18], 0.0
    )
    ms_ref[...] = jnp.sum(mixes, axis=0, keepdims=True)


def route_call(x, att, ow, sw, gain, res, rt, tc, tr, slots):
    t = x.shape[0]
    part = min(slots, 256)
    return pl.pallas_call(
        route_body,
        grid=(slots // part,),
        in_specs=[
            whole((t, D)), whole((t, D)), whole((D, D)), whole((D, LANES)), whole((1, D)),
            whole((t, LANES)), whole((t, 2)), whole((t, 2)), whole((2, t)),
        ],
        out_specs=[
            whole((t, D)), whole((t, D)), whole((t, LANES)),
            spec((part, D), lambda i: (i, 0)),
            spec((1, part), lambda i: (0, i)),
        ],
        out_shape=[
            shape((t, D), F32), shape((t, D), BF16), shape((t, LANES), F32),
            shape((slots, D), BF16), shape((1, slots), F32),
        ],
        name="route_dispatch",
        **params((2 * t * D * D + 2 * slots * t * D, 8 * t * D)),
    )(x, att, ow, sw, gain, res, rt, tc, tr)


def expert_fwd_body(x_ref, w_ref, o_ref, acc_ref):
    step = pl.program_id(0)
    x = x_ref[...]
    wide = w_ref.shape[-1]
    wg = w_ref[:, 0].reshape(D, wide)
    wu = w_ref[:, 1].reshape(D, wide)
    wd = w_ref[:, 2].reshape(D, wide)
    gate = dot(x, wg)
    up = dot(x, wu)
    act = (gate / (1.0 + jnp.exp(-gate)) * up).astype(BF16)
    out = dot_nt(act, wd)

    @pl.when(step == 0)
    def _():
        acc_ref[...] = out

    @pl.when(step > 0)
    def _():
        acc_ref[...] += out

    @pl.when(step == pl.num_programs(0) - 1)
    def _():
        o_ref[...] = acc_ref[...].astype(BF16)


def expert_fwd(xr, w):
    rows = xr.shape[0]
    shards, _, per, wide = w.shape
    part = min(wide, 256)
    return pl.pallas_call(
        expert_fwd_body,
        grid=(wide // part,),
        in_specs=[whole((rows, D)), spec((shards, 3, per, part), lambda i: (0, 0, 0, i))],
        out_specs=whole((rows, D)),
        out_shape=shape((rows, D), BF16),
        scratch_shapes=[pltpu.VMEM((rows, D), F32)],
        name="expert_forward",
        **params((6 * rows * D * wide, 6 * D * wide)),
    )(xr, w)


def expert_bwd_body(x_ref, g_ref, m_ref, w_ref, gi_ref, dw_ref, acc_ref, xt_ref, gl_ref, gt_ref):
    step = pl.program_id(0)

    @pl.when(step == 0)
    def _():
        low = (g_ref[...].astype(F32) * m_ref[...]).astype(BF16)
        gl_ref[...] = low
        gt_ref[...] = low.T
        xt_ref[...] = x_ref[...].T

    x = x_ref[...]
    g = gl_ref[...]
    shards, _, per, wide = w_ref.shape
    wg = w_ref[:, 0].reshape(D, wide)
    wu = w_ref[:, 1].reshape(D, wide)
    wd = w_ref[:, 2].reshape(D, wide)
    gate = dot(x, wg)
    up = dot(x, wu)
    sig = 1.0 / (1.0 + jnp.exp(-gate))
    silu = gate * sig
    act = (silu * up).astype(BF16)
    ga = dot(g, wd)
    d_gate = (ga * up * sig * (1.0 + gate * (1.0 - sig))).astype(BF16)
    d_up = (ga * silu).astype(BF16)
    gi = dot_nt(d_gate, wg) + dot_nt(d_up, wu)

    @pl.when(step == 0)
    def _():
        acc_ref[...] = gi

    @pl.when(step > 0)
    def _():
        acc_ref[...] += gi

    xt = xt_ref[...]
    dw_ref[:, 0] = dot(xt, d_gate).astype(BF16).reshape(shards, per, wide)
    dw_ref[:, 1] = dot(xt, d_up).astype(BF16).reshape(shards, per, wide)
    dw_ref[:, 2] = dot(gt_ref[...], act).astype(BF16).reshape(shards, per, wide)

    @pl.when(step == pl.num_programs(0) - 1)
    def _():
        gi_ref[...] = acc_ref[...].astype(BF16)


def expert_bwd(xr, gr, mix, w):
    rows = xr.shape[0]
    shards, _, per, wide = w.shape
    part = min(wide, 256)
    wspec = spec((shards, 3, per, part), lambda i: (0, 0, 0, i))
    return pl.pallas_call(
        expert_bwd_body,
        grid=(wide // part,),
        in_specs=[whole((rows, D)), whole((rows, D)), whole((rows, 1)), wspec],
        out_specs=[whole((rows, D)), wspec],
        out_shape=[shape((rows, D), BF16), shape(w.shape, BF16)],
        scratch_shapes=[
            pltpu.VMEM((rows, D), F32),
            pltpu.VMEM((D, rows), BF16),
            pltpu.VMEM((rows, D), BF16),
            pltpu.VMEM((D, rows), BF16),
        ],
        name="expert_backward",
        **params((16 * rows * D * wide, 12 * D * wide)),
    )(xr, gr, mix, w)


def mix_body(
    h_ref, g_ref, pr_ref, rt_ref, tc_ref, ret_ref, n_ref, sw_ref, rows_ref,
    out_ref, gn_ref, gl_ref, gs_ref,
):
    t = h_ref.shape[0]
    slots = ret_ref.shape[0]
    hidden = h_ref[...]
    g16 = g_ref[...]
    g = g16.astype(F32)
    pr = pr_ref[...]
    scale = lax.rsqrt(jnp.mean(hidden * hidden, axis=-1, keepdims=True) + EPS)
    normed = hidden * scale * rows_ref[2:3, :]
    lane = lax.broadcasted_iota(jnp.int32, (t, LANES), 1)
    slot = lax.broadcasted_iota(jnp.int32, (t, slots), 1)
    first = EXPERTS + 4
    ret = ret_ref[...]
    c0 = [pr[:, first + 2 * k : first + 2 * k + 1] for k in range(2)]
    c1 = [pr[:, first + 2 * k + 1 : first + 2 * k + 2] for k in range(2)]
    total = hidden
    s = jnp.zeros((t, LANES), F32)
    coef = jnp.zeros((t, 1), F32)
    weight = [jnp.zeros((t, 1), F32) for _ in range(2)]
    for j in range(2):
        route = rt_ref[:, j : j + 1]
        mix = pr[:, 16 + j : 17 + j]
        branch = dot((slot == tc_ref[:, j : j + 1]).astype(BF16), ret)
        keep = jnp.where(route == EXPERTS + 1, 1.0, 0.0)
        for k in range(2):
            here = jnp.where(route == EXPERTS + 2 + k, 1.0, 0.0)
            keep = keep + here * c0[k]
            weight[k] = weight[k] + here * mix
            branch = branch + (here * c1[k]) * rows_ref[k : k + 1, :]
        branch = branch + keep * normed
        coef = coef + mix * keep
        total = total + mix * branch
        gp = jnp.sum(g * branch, axis=-1, keepdims=True)
        s = s + jnp.where(lane == route, gp, 0.0)
    out_ref[...] = total.astype(BF16)
    probs = jnp.where(lane < first, pr, 0.0)
    d_logits = probs * (s - jnp.sum(probs * s, axis=-1, keepdims=True))
    gl_ref[...] = d_logits
    dz = d_logits
    dvec = jnp.zeros((t, LANES), F32)
    g_dot_n = jnp.sum(g * normed, axis=-1, keepdims=True)
    for k in range(2):
        d0 = weight[k] * g_dot_n
        d1 = weight[k] * jnp.sum(g * rows_ref[k : k + 1, :], axis=-1, keepdims=True)
        mean = c0[k] * d0 + c1[k] * d1
        dz = jnp.where(lane == first + 2 * k, c0[k] * (d0 - mean), dz)
        dz = jnp.where(lane == first + 2 * k + 1, c1[k] * (d1 - mean), dz)
        dvec = jnp.where(lane == 16 + k, weight[k] * c1[k], dvec)
    hi, lo = split_hi_lo(dz)
    sw = sw_ref[...]
    gn_ref[...] = coef * g + (dot_nt(hi, sw) + dot_nt(lo, sw))
    nt = n_ref[...].T
    gt = g16.T
    vhi, vlo = split_hi_lo(dvec)
    gs = dot(nt, hi) + dot(nt, lo) + dot(gt, vhi) + dot(gt, vlo)

    @pl.when(pl.program_id(0) == 0)
    def _():
        gs_ref[...] = gs

    @pl.when(pl.program_id(0) > 0)
    def _():
        gs_ref[...] += gs


def mix_call(hidden, g, pr, rt, tc, ret, low, sw, rows):
    t = hidden.shape[0]
    half = t // 2
    slots = ret.shape[0]
    tile = spec((half, D), lambda i: (i, 0))
    lane_tile = spec((half, LANES), lambda i: (i, 0))
    pair = spec((half, 2), lambda i: (i, 0))
    return pl.pallas_call(
        mix_body,
        grid=(2,),
        in_specs=[
            tile, tile, lane_tile, pair, pair, whole((slots, D)), tile, whole((D, LANES)),
            whole((8, D)),
        ],
        out_specs=[tile, tile, lane_tile, whole((D, LANES))],
        out_shape=[
            shape((t, D), BF16), shape((t, D), F32), shape((t, LANES), F32), shape((D, LANES), F32),
        ],
        name="mixture",
        **params((4 * t * slots * D, 12 * t * D)),
    )(hidden, g, pr, rt, tc, ret, low, sw, rows)


def norm_back_body(
    h_ref, g_ref, gn_ref, tc_ref, ret_ref, rows_ref, ow_ref, att_ref,
    gh_ref, do_ref, dot_ref, gow_ref, gg_ref,
):
    t = h_ref.shape[0]
    slots = ret_ref.shape[0]
    hidden = h_ref[...]
    slot = lax.broadcasted_iota(jnp.int32, (t, slots), 1)
    pick = (slot == tc_ref[:, 0:1]) | (slot == tc_ref[:, 1:2])
    gn = gn_ref[...] + dot(pick.astype(BF16), ret_ref[...])
    q = lax.rsqrt(jnp.mean(hidden * hidden, axis=-1, keepdims=True) + EPS)
    u = gn * rows_ref[2:3, :]
    mean = jnp.mean(u * hidden, axis=-1, keepdims=True)
    gh = g_ref[...].astype(F32) + q * u - hidden * (q * q * q * mean)
    gh_ref[...] = gh
    gb = gh.astype(BF16)
    d_out = dot_nt(gb, ow_ref[...])
    do_ref[...] = d_out.astype(BF16)
    dot_ref[...] = d_out.T.astype(BF16)
    gow = dot(att_ref[...].T, gb)
    gain = jnp.sum(gn * hidden * q, axis=0, keepdims=True)

    @pl.when(pl.program_id(0) == 0)
    def _():
        gow_ref[...] = gow
        gg_ref[...] = jnp.broadcast_to(gain, gg_ref.shape)

    @pl.when(pl.program_id(0) > 0)
    def _():
        gow_ref[...] += gow
        gg_ref[...] += jnp.broadcast_to(gain, gg_ref.shape)


def norm_back_call(hidden, g, gn, tc, ret, rows, ow, att):
    t = hidden.shape[0]
    half = t // 2 if (t // 2) % LANES == 0 else t
    slots = ret.shape[0]
    tile = spec((half, D), lambda i: (i, 0))
    return pl.pallas_call(
        norm_back_body,
        grid=(t // half,),
        in_specs=[
            tile, tile, tile, spec((half, 2), lambda i: (i, 0)), whole((slots, D)), whole((8, D)),
            whole((D, D)), tile,
        ],
        out_specs=[tile, tile, spec((D, half), lambda i: (0, i)), whole((D, D)), whole((8, D))],
        out_shape=[
            shape((t, D), F32), shape((t, D), BF16), shape((D, t), BF16), shape((D, D), F32),
            shape((8, D), F32),
        ],
        name="norm_two_back",
        **params((2 * t * slots * D + 4 * t * D * D, 16 * t * D)),
    )(hidden, g, gn, tc, ret, rows, ow, att)


def qkv_back_body(
    x_ref, n_ref, dq_ref, dkv_ref, gh_ref, c_ref, s_ref, w_ref, gain_ref,
    gi_ref, gw_ref, gg_ref, gq_ref,
):
    cosine = c_ref[...]
    sine = s_ref[...]
    for i in range(PAIRS):
        cols = slice(i * LANES, (i + 1) * LANES)
        v = dq_ref[:, cols]
        gq_ref[:, cols] = (v * cosine - partner(v) * sine).astype(BF16)
        v = dkv_ref[:, 2 * i * LANES : (2 * i + 1) * LANES]
        gq_ref[:, D + i * LANES : D + (i + 1) * LANES] = (v * cosine - partner(v) * sine).astype(BF16)
        v = dkv_ref[:, (2 * i + 1) * LANES : (2 * i + 2) * LANES]
        gq_ref[:, 2 * D + i * LANES : 2 * D + (i + 1) * LANES] = v.astype(BF16)
    gq = gq_ref[...]
    gn = dot_nt(gq, w_ref[...])
    x = x_ref[...].astype(F32)
    q = lax.rsqrt(jnp.mean(x * x, axis=-1, keepdims=True) + EPS)
    u = gn * gain_ref[...]
    mean = jnp.mean(u * x, axis=-1, keepdims=True)
    gi_ref[...] = gh_ref[...] + q * u - x * (q * q * q * mean)
    gain = jnp.sum(gn * x * q, axis=0, keepdims=True)
    nt = n_ref[...].T
    start = pl.program_id(0) == 0
    for c in range(3):
        cols = slice(c * D, (c + 1) * D)
        gw = dot(nt, gq[:, cols])

        @pl.when(start)
        def _():
            gw_ref[:, cols] = gw

        @pl.when(jnp.logical_not(start))
        def _():
            gw_ref[:, cols] += gw

    @pl.when(start)
    def _():
        gg_ref[...] = jnp.broadcast_to(gain, gg_ref.shape)

    @pl.when(jnp.logical_not(start))
    def _():
        gg_ref[...] += jnp.broadcast_to(gain, gg_ref.shape)


def qkv_back_call(x, low, dq, dkv, gh, cosine, sine, pack, gain):
    t = x.shape[0]
    half = t // 2
    tile = spec((half, D), lambda i: (i, 0))
    lane_tile = spec((half, LANES), lambda i: (i, 0))
    return pl.pallas_call(
        qkv_back_body,
        grid=(2,),
        in_specs=[
            tile, tile, tile, spec((half, 2 * D), lambda i: (i, 0)), tile, lane_tile, lane_tile,
            whole((D, 3 * D)), whole((1, D)),
        ],
        out_specs=[tile, whole((D, 3 * D)), whole((8, D))],
        out_shape=[shape((t, D), F32), shape((D, 3 * D), F32), shape((8, D), F32)],
        scratch_shapes=[pltpu.VMEM((half, 3 * D), BF16)],
        name="qkv_back",
        **params((4 * t * D * 3 * D, 20 * t * D)),
    )(x, low, dq, dkv, gh, cosine, sine, pack, gain)


def rotation_tables(position):
    half = HEAD_DIM // 2
    frequency = 10000.0 ** (-jnp.arange(half, dtype=F32) / half)
    angles = position[:, None] * frequency[None, :]
    cosine, sine = jnp.cos(angles), jnp.sin(angles)
    return (
        jnp.concatenate([cosine] * 4, axis=1),
        jnp.concatenate([-sine, sine, -sine, sine], axis=1),
    )


def to_rows(array):
    return jnp.transpose(array, (1, 0, 2)).reshape(2 * array.shape[0], array.shape[2])


def from_rows(array):
    r = array.shape[0] // 2
    return jnp.transpose(array.reshape(2, r, array.shape[1]), (1, 0, 2))


def per_device(
    hidden_in, cotangent, gate_residual, routes, groups, lengths, attn_gain, qkv_weight, out_weight,
    ffn_gain, router_weight, const_proj, const_vec, gate_weight, up_weight, down_weight,
):
    del groups
    r = hidden_in.shape[0]
    t = 2 * r
    capacity = r // 2
    owners = lax.axis_size("expert")
    copies = owners // EXPERTS
    slots = EXPERTS * capacity
    me = lax.axis_index("expert")
    per_cont = max(CONT_LEN // r, 1)

    small = jnp.concatenate(
        [
            router_weight, const_proj, const_vec, attn_gain[:, None], ffn_gain[:, None],
            jnp.zeros((attn_gain.shape[0], LANES - 20), BF16),
        ],
        axis=1,
    )
    pack = lax.all_gather(
        jnp.concatenate([qkv_weight, out_weight, small], axis=1), ALL_AXES, axis=0, tiled=True
    )
    out_w = pack[:, 3 * D : 4 * D]
    small_w = pack[:, 4 * D :]
    small_rows = jnp.transpose(small_w[:, 16:24]).astype(F32)
    gain_one = small_rows[2:3]
    rows_two = jnp.concatenate([small_rows[0:2], small_rows[3:4], small_rows[3:8]], axis=0)
    gain_two = small_rows[3:4]

    index = jnp.arange(r, dtype=jnp.int32)
    row_ids = me * r + index
    position = jnp.concatenate([row_ids, PROMPT + row_ids % CONT_LEN]).astype(F32)
    cosine, sine = rotation_tables(position)
    cont = (me * r) // CONT_LEN
    length = lax.dynamic_slice(lengths, (cont,), (1,))
    header = jnp.stack([me, (me * r) % CONT_LEN]).astype(jnp.int32)
    header = jnp.concatenate([header, length.astype(jnp.int32)])
    sc = jnp.concatenate([header, jnp.arange(owners, dtype=jnp.int32)])

    picked = to_rows(routes)
    flat = jnp.transpose(picked).reshape(2 * t)
    hot = flat[:, None] == jnp.arange(EXPERTS, dtype=jnp.int32)[None, :]
    earlier = jnp.arange(2 * t)[:, None] > jnp.arange(2 * t)[None, :]
    before = jnp.dot(earlier.astype(BF16), hot.astype(BF16), preferred_element_type=F32)
    slot_index = jnp.sum(jnp.where(hot, before, 0.0), axis=1).astype(jnp.int32)
    target = jnp.where(flat < EXPERTS, flat * capacity + slot_index, -1)
    target_rows = target.reshape(2, t)
    target_cols = jnp.transpose(target_rows)

    def to_owners(rows):
        w = rows.shape[-1]
        shaped = rows.reshape(EXPERTS, 1, capacity, w)
        return jnp.broadcast_to(shaped, (EXPERTS, copies, capacity, w)).reshape(owners, capacity, w)

    def exchange(rows):
        got = lax.all_to_all(rows, "expert", split_axis=0, concat_axis=0, tiled=True)
        return got.reshape(owners * got.shape[1], got.shape[2])

    def from_owners(rows):
        got = exchange(rows.reshape(owners, capacity, D))
        if copies == 1:
            return got
        got = got.reshape(EXPERTS, copies, capacity, D).astype(F32)
        return jnp.sum(got, axis=1).reshape(slots, D).astype(BF16)

    x = to_rows(hidden_in)
    g = to_rows(cotangent)
    slot_ids = jnp.arange(slots, dtype=jnp.int32)[:, None]
    placement = (slot_ids == target_rows[0][None, :]) | (slot_ids == target_rows[1][None, :])
    g_send = jnp.dot(placement.astype(BF16), g, preferred_element_type=F32).astype(BF16)
    g_got = exchange(to_owners(g_send))

    low_one, q, q_t, kv = qkv_call(x, gain_one, pack, cosine, sine)
    kv_prompt = kv[:r]
    kv_all = lax.all_gather(kv_prompt, "expert", axis=0, tiled=True)
    if per_cont == 1:
        kv_own = kv[r:]
    else:
        cont_groups = [
            [c * per_cont + i for i in range(per_cont)] for c in range(owners // per_cont)
        ]
        kv_own = lax.all_gather(
            kv[r:], "expert", axis=0, tiled=True, axis_index_groups=cont_groups
        )
    weights = lax.all_gather(
        jnp.stack([gate_weight, up_weight, down_weight]), "dp", axis=0, tiled=False
    )
    st, acc = fwd_local(sc, q_t, kv_prompt, kv_own)
    st, att_t, att = fwd_remote(sc, q_t, kv_all, st, acc, True)

    res = jnp.pad(to_rows(gate_residual), ((0, 0), (0, LANES - EXPERTS - 4)))
    hidden, low_two, pr, x_send, mix_send = route_call(
        x, att, out_w, small_w, gain_two, res, picked, target_cols, target_rows, slots
    )
    x_got = exchange(to_owners(x_send))
    mix_got = lax.all_to_all(
        to_owners(mix_send.reshape(EXPERTS, capacity, 1)).reshape(owners, capacity),
        "expert", split_axis=0, concat_axis=0, tiled=True,
    ).reshape(owners * capacity, 1)
    out_back = from_owners(expert_fwd(x_got, weights))
    grad_in, grad_w = expert_bwd(x_got, g_got, mix_got, weights)
    in_back = from_owners(grad_in)
    output, gn, grad_logits, grad_small = mix_call(
        hidden, g, pr, picked, target_cols, out_back, low_two, small_w, rows_two
    )
    grad_expert = lax.psum_scatter(
        grad_w.reshape(-1, grad_w.shape[-1]), "dp", scatter_dimension=0, tiled=True
    ).astype(F32)
    gh, d_att, d_att_t, grad_ow, gg_two = norm_back_call(
        hidden, g, gn, target_cols, in_back, rows_two, out_w, att
    )

    st, dq_t, dkv_own_prompt, dkv_cont = bwd_local(
        sc, q_t, q, d_att_t, d_att, st, att_t, kv_prompt, kv_own
    )
    _, dkv_all, dq = bwd_remote(sc, q_t, q, d_att_t, d_att, st, dq_t, kv_all, True)
    dkv_prompt = lax.psum_scatter(dkv_all, "expert", scatter_dimension=0, tiled=True)
    if per_cont > 1:
        dkv_cont = lax.psum_scatter(
            dkv_cont, "expert", scatter_dimension=0, tiled=True, axis_index_groups=cont_groups
        )
    dkv = jnp.concatenate([dkv_prompt.astype(F32) + dkv_own_prompt, dkv_cont], axis=0)
    grad_input, grad_qkv, gg_one = qkv_back_call(
        x, low_one, dq, dkv, gh, cosine, sine, pack, gain_one
    )

    last = jnp.concatenate(
        [
            grad_small[:, :18], jnp.transpose(gg_one[0:1]), jnp.transpose(gg_two[0:1]),
            jnp.zeros((D, LANES - 20), F32),
        ],
        axis=1,
    )
    dense = lax.psum_scatter(
        jnp.concatenate([grad_qkv, grad_ow, last], axis=1).astype(BF16),
        ALL_AXES, scatter_dimension=0, tiled=True,
    ).astype(F32)
    tail = dense[:, 4 * D :]
    per = grad_expert.shape[0] // 3
    return (
        from_rows(output),
        from_rows(grad_input),
        from_rows(grad_logits)[:, :, : EXPERTS + 4],
        tail[:, 18],
        dense[:, : 3 * D],
        dense[:, 3 * D : 4 * D],
        tail[:, 19],
        tail[:, :12],
        tail[:, 12:16],
        tail[:, 16:18],
        grad_expert[:per],
        grad_expert[per : 2 * per],
        grad_expert[2 * per :],
    )


def solution(mesh):
    rows = P(ALL_AXES, None, None)
    flat = P(ALL_AXES)
    mat = P(ALL_AXES, None)
    expert = P("dp", "expert")
    in_specs = (
        rows, rows, rows, rows, P("dp"), P("dp"), flat, mat, mat, flat, mat, mat, mat,
        expert, expert, expert,
    )
    out_specs = (
        rows, rows, rows, flat, mat, mat, flat, mat, mat, mat, expert, expert, expert,
    )
    return jax.shard_map(
        per_device, mesh=mesh, in_specs=in_specs, out_specs=out_specs, check_vma=False
    )
```

time: 2090 us -> 812 us (0.39)
  matrix products: 443 us -> 2.73 us
  local copies, waits for them, and re-layouts: 488 us -> 54.4 us
  blocking collectives: 295 us -> 44.5 us
  Pallas kernels: 0 us -> 208 us
  waiting for transfers between devices: 640 us -> 445 us
  other arithmetic: 160 us -> 15.8 us
    dot_general x79 -> x2, matrix products: 443 us -> 2.73 us  [the longest x1 2.26 us: per_device(): jnp.dot(placement.astype(BF16), g, preferred_element_type=F32).astype(BF16)]
    reduce_scatter x6 -> x2, waiting for transfers between devices: 436 us -> 162 us  [the longest x1 122 us: per_device(): lax.psum_scatter(dkv_all, 'expert', scatter_dimension=0, tiled=True)]
    all_gather x3 -> x0, blocking collectives: 213 us -> none  [the longest x1 82.8 us: per_device(): lax.all_gather(const_vec, ('dp', 'expert'), axis=0, tiled=True)]
    pallas_call x0 -> x11, Pallas kernels: none -> 208 us  [the longest x1 48.2 us: expert_bwd(): pl.pallas_call(expert_bwd_body, grid=(wide // part,), in_specs=[whole((ro...]
    unnamed x12 -> x7, waiting for transfers between devices: 2.59 us -> 103 us
    cond x88 -> x0, local copies, waits for them, and re-layouts: 97.3 us -> none
    reshape x60 -> x4, local copies, waits for them, and re-layouts: 102 us -> 5.23 us  [the longest x3 4.19 us: from_rows(): return jnp.transpose(array.reshape(2, r, array.shape[1]), (1, 0, 2))]
    reduce_sum x37 -> x0, other arithmetic: 84.2 us -> none  [the longest x8 25.2 us: fold_compute(): weight_sum = weight_sum * factor + jnp.sum(weight_matrix, axis=-1)]
  transfers between devices with their start and end apart: 16 -> 10, of which waited for: 10 -> 6; matrix products, arithmetic and copies ran while one was open for 25% -> 6% of each run, Pallas kernels for 0% -> 18%
where the time goes in v1:
time: 812 us; the launch traced here: 806 us
  waiting for transfers between devices  445 us (55%)
  Pallas kernels  208 us (26%)
  local copies, waits for them, and re-layouts  54.4 us (7%)
  blocking collectives  44.5 us (5%)
  starting transfers between devices  20.8 us (3%)
  other arithmetic  15.8 us (2%)
  between operations  14.7 us (2%)
    reduce_scatter x1, waiting for transfers between devices, per_device(): lax.psum_scatter(dkv_all, 'expert', scatter_dimension=0, tiled=True)  122 us
    unnamed x7, waiting for transfers between devices  103 us
    all_gather x1, waiting for transfers between devices, per_device(): kv_all = lax.all_gather(kv_prompt, 'expert', axis=0, tiled=True)  95.2 us
    all_gather x1, waiting for transfers between devices, per_device(): lax.all_gather(jnp.concatenate([qkv_weight, out_weight, small], axis=1),...  62.1 us
    pallas_call x1, Pallas kernels, expert_bwd(): pl.pallas_call(expert_bwd_body, grid=(wide // part,), in_specs=[whole((ro...  48.2 us
    all_to_all x1, blocking collectives, exchange(): lax.all_to_all(rows, 'expert', split_axis=0, concat_axis=0, tiled=True)  44.5 us
    reduce_scatter x1, waiting for transfers between devices, per_device(): lax.psum_scatter(grad_w.reshape(-1, grad_w.shape[-1]), 'dp', scatter_dime...  40.3 us
    pallas_call x1, Pallas kernels, bwd_remote(): pl.pallas_call(functools.partial(bwd_remote_body, rows // (t // 2), final...  31.7 us
  transfers between devices with their start and end apart: 10, of which 6 were waited for; matrix products, arithmetic and copies ran while one was open for 6% of the time, Pallas kernels for 18%

profile of v1, /device:TPU:0, one launch (start us, length us, event | category | flops | bytes accessed | tf_op | source)
XLA Modules:
  0.0 806.0 jit_solution(6507874193672798248)
XLA Ops:
  12.7 2.1 copy.98
  17.8 62.1 %all-gather.5.cloned.1.call-done.wq_ref.wk_ref.wv_ref.w_ref = bf16[768,3200]{1,0:T(8,128)(2,1)} async-done(((bf16[24,3200]{1,0:T(8,128)(2,1)}), bf16[768,3200]{1,0:T(8,128)(2,1)}) %all-gather.5.cloned.1.call-update) | async-done | bytes 4915216 | tf_op jit(solution)/shard_map/all_gather | solution.py:882
  81.7 8.7 %qkv_rope.1 = (bf16[512,768]{1,0:T(8,128)(2,1)}, bf16[512,768]{1,0:T(8,128)(2,1)}, bf16[768,512]{1,0:T(8,128)(2,1)}, bf16[512,1536]{1,0:T(8,128)(2,1)}) custom-call(bf16[512,768]{1,0:T(8,128)(2,1)} %bitcast.54, f32[1,768]{1,0:T(1,128)} %get-tuple-element.141.gain_ref, bf16[768,3200]{1,0:T(8,128)(2,1)} %all-gather.5.cloned.1.call-done.wq_ref.wk_ref.wv_ref.w_ref, ...), custom_call_target="tpu_custom_call" | custom-call | flops 1811939328 | bytes 3538944 | tf_op jit(solution)/shard_map/qkv_rope/pallas_call | solution.py:97
  90.4 2.8 fusion.18
  96.8 2.3 fusion.4
  99.0 4.2 all-to-all-start.2
  106.9 2.4 slice.115.ow_ref
  110.9 12.4 %attend_local.1 = (f32[48,512]{1,0:T(8,128)}, f32[768,512]{1,0:T(8,128)}) custom-call(s32[11]{0:T(128)} %pad_add_fusion.sc_ref, bf16[768,512]{1,0:T(8,128)(2,1)} %get-tuple-element.47.qt_ref, bf16[256,1536]{1,0:T(8,128)(2,1)} %get-tuple-element.139.kv_ref, bf16[256,1536]{1,0:T(8,128)(2,1)} %get-tuple-element.138.kvo_ref), custom_call_target="tpu_custom_call" | custom-call | flops 1610612736 | bytes 1572864 | tf_op jit(solution)/shard_map/attend_local/pallas_call | solution.py:241
  123.4 95.2 %all-gather.7.cloned.1.call-done.kv_ref = bf16[2048,1536]{1,0:T(8,128)(2,1)} async-done(((bf16[256,1536]{1,0:T(8,128)(2,1)}), bf16[2048,1536]{1,0:T(8,128)(2,1)}) %all-gather.7.cloned.1.call-update) | async-done | bytes 6291472 | tf_op jit(solution)/shard_map/all_gather | solution.py:937
  218.5 30.6 %attend_remote.1 = (f32[48,512]{1,0:T(8,128)}, f32[768,512]{1,0:T(8,128)}, bf16[512,768]{1,0:T(8,128)(2,1)}) custom-call(s32[11]{0:T(128)} %pad_add_fusion.sc_ref, bf16[768,512]{1,0:T(8,128)(2,1)} %get-tuple-element.47.qt_ref, bf16[2048,1536]{1,0:T(8,128)(2,1)} %all-gather.7.cloned.1.call-done.kv_ref, f32[48,512]{1,0:T(8,128)} %get-tuple-element.49.st_in, ...), custom_call_target="tpu_custom_call" | custom-call | flops 12884901888 | bytes 9437184 | tf_op jit(solution)/shard_map/attend_remote/pallas_call | solution.py:265
  249.1 9.6 %route_dispatch.1 = (f32[512,768]{1,0:T(8,128)}, bf16[512,768]{1,0:T(8,128)(2,1)}, f32[512,128]{1,0:T(8,128)}, bf16[1024,768]{1,0:T(8,128)(2,1)}, f32[1,1024]{1,0:T(1,128)}) custom-call(bf16[512,768]{1,0:T(8,128)(2,1)} %bitcast.55, bf16[512,768]{1,0:T(8,128)(2,1)} %get-tuple-element.51.att_ref, bf16[768,768]{1,0:T(8,128)(2,1)} %slice.115.ow_ref, ...), custom_call_target="tpu_custom_call" | custom-call | flops 1409286144 | bytes 3145728 | tf_op jit(solution)/shard_map/route_dispatch/pallas_call | solution.py:502
  258.7 44.5 %all_to_all.29 = bf16[8,128,768]{2,1,0:T(8,128)(2,1)} all-to-all(bf16[8,128,768]{2,1,0:T(8,128)(2,1)} %bitcast.74), channel_id=1, replica_groups=mesh['dp'=4,'expert'=8] {'expert'}, dimensions={0} | all-to-all | bytes 3145728 | tf_op jit(solution)/shard_map/all_to_all | solution.py:918
  303.3 3.9 all-to-all-start.3
  307.2 17.6 %expert_forward.1 = bf16[1024,768]{1,0:T(8,128)(2,1)} custom-call(bf16[1024,768]{1,0:T(8,128)(2,1)} %bitcast.71, bf16[4,3,192,2048]{3,2,1,0:T(8,128)(2,1)} %bitcast.93), custom_call_target="tpu_custom_call" | custom-call | flops 9663676416 | bytes 9437184 | tf_op jit(solution)/shard_map/expert_forward/pallas_call | solution.py:552
  324.9 6.0 all-to-all-start.1
  331.9 48.2 %expert_backward.1 = (bf16[1024,768]{1,0:T(8,128)(2,1)}, bf16[4,3,192,2048]{3,2,1,0:T(8,128)(2,1)}) custom-call(bf16[1024,768]{1,0:T(8,128)(2,1)} %bitcast.72, bf16[1024,768]{1,0:T(8,128)(2,1)} %bitcast.66, f32[1024,1]{1,0:T(8,128)} %copy.114.m_ref, bf16[4,3,192,2048]{3,2,1,0:T(8,128)(2,1)} %bitcast.94), custom_call_target="tpu_custom_call" | custom-call | flops 25769803776 | bytes 18874368 | tf_op jit(solution)/shard_map/expert_backward/pallas_call | solution.py:613
  381.3 6.0 all-to-all-start.4
  388.5 12.2 %mixture.1 = (bf16[512,768]{1,0:T(8,128)(2,1)}, f32[512,768]{1,0:T(8,128)}, f32[512,128]{1,0:T(8,128)}, f32[768,128]{1,0:T(8,128)}) custom-call(f32[512,768]{1,0:T(8,128)} %get-tuple-element.52.h_ref, bf16[512,768]{1,0:T(8,128)(2,1)} %bitcast.58, f32[512,128]{1,0:T(8,128)} %get-tuple-element.53.pr_ref, s32[512,2]{1,0:T(8,128)} %bitcast.65, ...), custom_call_target="tpu_custom_call" | custom-call | flops 1610612736 | bytes 4718592 | tf_op jit(solution)/shard_map/mixture/pallas_call | solution.py:705
  400.7 22.3 %all-to-all-done.4 = bf16[8,128,768]{2,1,0:T(8,128)(2,1)S(1)} async-done(((bf16[8,128,768]{2,1,0:T(8,128)(2,1)}), bf16[8,128,768]{2,1,0:T(8,128)(2,1)S(1)}, u32[]{:S(2)}, u32[]{:S(2)}) %all-to-all-start.4) | async-done | bytes 1572896 | tf_op jit(solution)/shard_map/all_to_all | solution.py:918
  424.2 8.9 %norm_two_back.1 = (f32[512,768]{1,0:T(8,128)}, bf16[512,768]{1,0:T(8,128)(2,1)}, bf16[768,512]{1,0:T(8,128)(2,1)}, f32[768,768]{1,0:T(8,128)}, f32[8,768]{1,0:T(8,128)}) custom-call(f32[512,768]{1,0:T(8,128)} %get-tuple-element.52.h_ref, bf16[512,768]{1,0:T(8,128)(2,1)} %bitcast.59, f32[512,768]{1,0:T(8,128)} %get-tuple-element.59.gn_ref, ...), custom_call_target="tpu_custom_call" | custom-call | flops 2013265920 | bytes 6291456 | tf_op jit(solution)/shard_map/norm_two_back/pallas_call | solution.py:759
  433.1 12.3 %attend_back_local.1 = (f32[48,512]{1,0:T(8,128)}, f32[768,512]{1,0:T(8,128)}, f32[256,1536]{1,0:T(8,128)}, f32[256,1536]{1,0:T(8,128)}) custom-call(s32[11]{0:T(128)} %pad_add_fusion.sc_ref, bf16[768,512]{1,0:T(8,128)(2,1)} %get-tuple-element.47.qt_ref, bf16[512,768]{1,0:T(8,128)(2,1)} %get-tuple-element.58.q_ref, ...), custom_call_target="tpu_custom_call" | custom-call | flops 4026531840 | bytes 6291456 | tf_op jit(solution)/shard_map/attend_back_local/pallas_call | solution.py:403
  445.3 31.7 %attend_back_remote.1 = (f32[768,512]{1,0:T(8,128)}, bf16[2048,1536]{1,0:T(8,128)(2,1)}, f32[512,768]{1,0:T(8,128)}) custom-call(s32[11]{0:T(128)} %pad_add_fusion.sc_ref, bf16[768,512]{1,0:T(8,128)(2,1)} %get-tuple-element.47.qt_ref, bf16[512,768]{1,0:T(8,128)(2,1)} %get-tuple-element.58.q_ref, bf16[768,512]{1,0:T(8,128)(2,1)} %get-tuple-element.62.dot_ref, ...), custom_call_target="tpu_custom_call" | custom-call | flops 32212254720 | bytes 18874368 | tf_op jit(solution)/shard_map/attend_back_remote/pallas_call | solution.py:438
  482.2 121.7 %reduce-scatter.6.cloned.1.call-done = bf16[256,1536]{1,0:T(8,128)(2,1)} async-done(((bf16[2048,1536]{1,0:T(8,128)(2,1)}), bf16[256,1536]{1,0:T(8,128)(2,1)}) %reduce-scatter.6.cloned.1.call-update) | async-done | bytes 786448 | tf_op jit(solution)/shard_map/reduce_scatter | solution.py:979
  603.9 1.9 convert_add_fusion
  606.0 1.8 pad_maximum_fusion.dkv_ref
  607.8 15.9 %qkv_back.1 = (f32[512,768]{1,0:T(8,128)}, f32[768,2304]{1,0:T(8,128)}, f32[8,768]{1,0:T(8,128)}) custom-call(bf16[512,768]{1,0:T(8,128)(2,1)} %bitcast.56, bf16[512,768]{1,0:T(8,128)(2,1)} %get-tuple-element.57.n_ref, f32[512,768]{1,0:T(8,128)} %get-tuple-element.68.dq_ref, f32[512,1536]{1,0:T(8,128)} %pad_maximum_fusion.dkv_ref, ...), custom_call_target="tpu_custom_call" | custom-call | flops 3623878656 | bytes 7864320 | tf_op jit(solution)/shard_map/qkv_back/pallas_call | solution.py:826
  623.8 3.4 convert.23
  629.4 7.9 concatenate.36
  640.9 2.4 copy.126
  643.3 40.3 %reduce-scatter.8.cloned.1.call-done = bf16[576,2048]{1,0:T(8,128)(2,1)} async-done(((bf16[2304,2048]{1,0:T(8,128)(2,1)}), bf16[576,2048]{1,0:T(8,128)(2,1)}) %reduce-scatter.8.cloned.1.call-update) | async-done | bytes 2359312 | tf_op jit(solution)/shard_map/reduce_scatter | solution.py:968
  683.6 4.0 fusion.17
  687.5 102.6 %reduce-scatter.10.cloned.1.call-done = bf16[24,3200]{1,0:T(8,128)(2,1)} async-done(((bf16[768,3200]{1,0:T(8,128)(2,1)}), bf16[24,3200]{1,0:T(8,128)(2,1)}) %reduce-scatter.10.cloned.1.call-update) | async-done | bytes 153616
  (116 shorter events, 43.5 us)
Async XLA Ops:
  7.2 72.7 %all-gather.5.cloned.1.call-start = ((), (), s32[]{:S(2)}) async-start(), calls=%async_computation.8 | async-start | bytes 5068800 | tf_op jit(solution)/shard_map/all_gather | solution.py:882
  12.7 205.8 %all-gather.7.cloned.1.call-start = ((), (), s32[]{:S(2)}) async-start(), calls=%async_computation.9 | async-start | bytes 7077888 | tf_op jit(solution)/shard_map/all_gather | solution.py:937
  90.4 2.9 copy-start.9
  90.4 2.9 copy-start.10
  90.4 2.9 copy-start.11
  93.2 214.0 %all-gather.9.cloned.1.call-start = ((), (), s32[]{:S(2)}) async-start(), calls=%async_computation.12 | async-start | bytes 11796480 | tf_op jit(solution)/shard_map/all_gather | solution.py:947
  95.0 0.7 copy-start.18
  95.0 1.1 copy-start.12
  95.9 7.6 copy-start.3
  96.3 2.8 copy-start.1
  99.0 5.2 copy-start.16
  99.0 159.7 %all-to-all-start.2 = ((bf16[8,128,768]{2,1,0:T(8,128)(2,1)}), bf16[8,128,768]{2,1,0:T(8,128)(2,1)S(1)}, u32[]{:S(2)}, u32[]{:S(2)}) async-start(bf16[8,128,768]{2,1,0:T(8,128)(2,1)} %bitcast.26), calls=%async_computation.2 | async-start | bytes 3145728 | tf_op jit(solution)/shard_map/all_to_all | solution.py:918
  103.2 1.1 copy-start.19
  103.5 5.8 copy-start.2
  258.7 44.6 %copy-start.5 = (bf16[8,128,768]{2,1,0:T(8,128)(2,1)}, bf16[8,128,768]{2,1,0:T(8,128)(2,1)S(1)}, u32[]{:S(2)}) copy-start(bf16[8,128,768]{2,1,0:T(8,128)(2,1)S(1)} %all-to-all-done.2) | copy-start | bytes 4718596
  303.3 21.6 %all-to-all-start.3 = ((f32[8,1,128]{2,1,0:T(1,128)}), f32[8,1,128]{2,1,0:T(1,128)S(1)}, u32[]{:S(2)}, u32[]{:S(2)}) async-start(f32[8,1,128]{2,1,0:T(1,128)} %bitcast.29), calls=%async_computation.3 | async-start | bytes 8192 | tf_op jit(solution)/shard_map/all_to_all | solution.py:958
  324.9 55.3 %all-to-all-start.1 = ((bf16[8,128,768]{2,1,0:T(8,128)(2,1)}), bf16[8,128,768]{2,1,0:T(8,128)(2,1)S(1)}, u32[]{:S(2)}, u32[]{:S(2)}) async-start(bf16[8,128,768]{2,1,0:T(8,128)(2,1)} %bitcast.73), calls=%async_computation.1 | async-start | bytes 3145728 | tf_op jit(solution)/shard_map/all_to_all | solution.py:918
  380.1 1.1 copy-start.6
  380.2 7.7 copy-start.17
  381.3 41.7 %all-to-all-start.4 = ((bf16[8,128,768]{2,1,0:T(8,128)(2,1)}), bf16[8,128,768]{2,1,0:T(8,128)(2,1)S(1)}, u32[]{:S(2)}, u32[]{:S(2)}) async-start(bf16[8,128,768]{2,1,0:T(8,128)(2,1)} %bitcast.70), calls=%async_computation.4 | async-start | bytes 3145728 | tf_op jit(solution)/shard_map/all_to_all | solution.py:918
  387.3 216.6 %reduce-scatter.6.cloned.1.call-start = ((), (), s32[]{:S(2)}) async-start(), calls=%async_computation.10 | async-start | bytes 7077888 | tf_op jit(solution)/shard_map/reduce_scatter | solution.py:979
  423.0 1.1 copy-start
  477.0 206.5 %reduce-scatter.8.cloned.1.call-start = ((), (), s32[]{:S(2)}) async-start(), calls=%async_computation.11 | async-start | bytes 11796480 | tf_op jit(solution)/shard_map/reduce_scatter | solution.py:968
  477.1 1.7 copy-start.4
  477.6 312.4 %reduce-scatter.10.cloned.1.call-start = ((), (), s32[]{:S(2)}) async-start(), calls=%async_computation.13 | async-start | bytes 5068800
  478.8 2.7 copy-start.15
  603.9 2.1 copy-start.8
  637.3 1.1 copy-start.13
  637.3 2.8 copy-start.14
  637.4 3.6 copy-start.7
Sparse Core Ops, SparseCore 0:
  12.8 67.0 all-gather.4
  93.4 125.1 all-gather.6
  220.1 62.4 all-gather.8
  477.2 126.6 reduce-scatter.5
  606.3 77.1 reduce-scatter.7
  689.1 100.9 reduce-scatter.9
